TPU v7x, 32 devices: a whole 2x2x4 slice. The times are simulated.
32 devices in a mesh: pairs: 2 (over y), col: 4 (over z), row: 4 (over x, core).
Axes of the slice: x: 2, y: 2, z: 4, core: 2. Of those that a mesh axis runs over, the one named last changes fastest.
Arguments:
- images: float32 [4, 8, 64, 512], P('pairs', None, 'row', 'col'), parts along dimension 0, may hold values from -12 to 12
- conv_weight: bfloat16 [32, 72], replicated, may hold values from -0.75 to 0.75
- conv_bias: float32 [32], replicated, may hold values from -2.5 to 2.5
- agg_weight: float32 [8, 27], replicated, may hold values from -3.2 to 3.2
Outputs:
- disparity: float32 [128, 512], P(('pairs', 'row'), 'col'), parts along dimension 0
There are 2 independent parts, one for each index of `pairs`. A program takes and returns all parts, laid end to end along the dimension named above; an argument that names none is the same for every part. Nothing has to cross between parts.
All inputs are finite; a program needn't handle non-finite values.
Results may differ from a plain program's by a relative error of at most 0.012.
The roundings to bfloat16 on the way count: a program that leaves them out, or rounds other values in their place, can miss the bound.
Values may be sent and summed in bfloat16 or wider, within the bound.
A program may use at most 64 MiB of HBM per device.

v0:
```python
import jax
import jax.numpy as jnp
from jax import lax
from jax.sharding import PartitionSpec as P

D = 64
DB = 16


def with_halo(shard, sides, width):
    for axis, dim in sides:
        devices, length = (lax.axis_size(axis), shard.shape[dim])
        up = [(i, (i + 1) % devices) for i in range(devices - 1)]
        down = [(j, i) for i, j in up]
        last = lax.slice_in_dim(shard, length - width, length, axis=dim)
        leading = lax.slice_in_dim(shard, 0, width, axis=dim)
        before = lax.ppermute(last, axis, up)
        after = lax.ppermute(leading, axis, down)
        shard = jnp.concatenate([before, shard, after], axis=dim)
    return shard


def from_behind(shard, axis, by):
    devices = lax.axis_size(axis)
    pairs = [(i, i + by) for i in range(devices) if 0 <= i + by < devices]
    return lax.ppermute(shard, axis, pairs)


def conv_valid(picture, conv_weight, conv_bias):
    height = picture.shape[1] - 2
    width_out = picture.shape[2] - 2
    patches = jnp.concatenate(
        [
            picture[:, step_y : step_y + height, step_x : step_x + width_out]
            for step_y in range(3)
            for step_x in range(3)
        ],
        axis=0,
    )
    flattened = patches.reshape(patches.shape[0], height * width_out)
    summed = (
        jnp.dot(conv_weight, flattened, preferred_element_type=jnp.float32) + conv_bias[:, None]
    )
    return jax.nn.leaky_relu(summed, 0.1).reshape(conv_weight.shape[0], height, width_out)


def inside(features, top_row, left_col, total_rows, total_cols):
    row_ids = top_row + lax.iota(jnp.int32, features.shape[1])
    col_ids = left_col + lax.iota(jnp.int32, features.shape[2])
    row_keep = jnp.logical_and(row_ids >= 0, row_ids < total_rows)
    col_keep = jnp.logical_and(col_ids >= 0, col_ids < total_cols)
    keeper = jnp.logical_and(row_keep[:, None], col_keep[None, :]).astype(jnp.float32)
    return (features * keeper[None]).astype(jnp.bfloat16)


def block_costs(left_feat, right_full, start_d, search, block_depth, groups):
    channels, height, width_out = left_feat.shape
    window = lax.dynamic_slice_in_dim(
        right_full, search - start_d - block_depth, width_out + block_depth + 1, 2
    )
    left_grouped = left_feat.reshape(groups, channels // groups, height, width_out)
    layers = []
    for offset in range(block_depth + 2):
        shifted = window[:, :, block_depth + 1 - offset : block_depth + 1 - offset + width_out]
        product = jnp.einsum(
            "gcyx,gcyx->gyx",
            left_grouped,
            shifted.reshape(groups, channels // groups, height, width_out),
            preferred_element_type=jnp.float32,
        ) * (groups / channels)
        disparity = start_d - 1 + offset
        usable = jnp.logical_and(disparity >= 0, disparity < search).astype(jnp.float32)
        layers.append((product * usable).astype(jnp.bfloat16))
    return jnp.stack(layers, axis=1)


def aggregate(cost_block, agg_weight, block_depth, height, width_out):
    tapped = jnp.einsum(
        "gdyx,gk->kdyx", cost_block.astype(jnp.float32), agg_weight, precision=lax.Precision.HIGHEST
    )
    summed = jnp.zeros((block_depth, height, width_out), jnp.float32)
    for step_d in range(3):
        for step_y in range(3):
            for step_x in range(3):
                summed = (
                    summed
                    + tapped[
                        9 * step_d + 3 * step_y + step_x,
                        step_d : step_d + block_depth,
                        step_y : step_y + height,
                        step_x : step_x + width_out,
                    ]
                )
    return summed


def softmax_update(running, scores, start_d):
    running_max, running_sum, running_moment = running
    values = (start_d + lax.iota(jnp.int32, scores.shape[0])).astype(jnp.float32)
    new_max = jnp.maximum(running_max, jnp.max(scores, axis=0))
    rescale = jnp.exp(running_max - new_max)
    weights = jnp.exp(scores - new_max[None])
    return (
        new_max,
        running_sum * rescale + jnp.sum(weights, axis=0),
        running_moment * rescale + jnp.sum(weights * values[:, None, None], axis=0),
    )


def on_device(images, conv_weight, conv_bias, agg_weight):
    pictures = images.astype(jnp.bfloat16)
    rows_here = pictures.shape[2]
    cols_here = pictures.shape[3]
    groups = agg_weight.shape[0]
    total_rows = rows_here * lax.axis_size("row")
    total_cols = cols_here * lax.axis_size("col")
    margin = 1
    padded = with_halo(pictures, (("col", 3), ("row", 2)), 2)
    top_row = lax.axis_index("row") * rows_here - margin
    left_col = lax.axis_index("col") * cols_here - margin
    left_feat = inside(
        conv_valid(padded[0], conv_weight, conv_bias), top_row, left_col, total_rows, total_cols
    )
    right_feat = inside(
        conv_valid(padded[1], conv_weight, conv_bias), top_row, left_col, total_rows, total_cols
    )
    strip_feat = from_behind(right_feat[:, :, cols_here - D : cols_here], "col", 1)
    channels = right_feat.shape[0]
    right_full = jnp.concatenate(
        [strip_feat, right_feat, jnp.zeros((channels, right_feat.shape[1], 1), jnp.bfloat16)],
        axis=2,
    )

    def advance(running, block_index):
        start_d = block_index * DB
        cost_block = block_costs(left_feat, right_full, start_d, D, DB, groups)
        scores = aggregate(cost_block, agg_weight, DB, rows_here, cols_here)
        return (softmax_update(running, scores, start_d), None)

    initial = (
        jnp.full((rows_here, cols_here), -1e30, jnp.float32),
        jnp.zeros((rows_here, cols_here), jnp.float32),
        jnp.zeros((rows_here, cols_here), jnp.float32),
    )
    running, unused = lax.scan(advance, initial, jnp.arange(D // DB, dtype=jnp.int32))
    return running[2] / running[1] / D


def solution(mesh):
    in_specs = (P("pairs", None, "row", "col"), P(), P(), P())
    out_specs = P(("pairs", "row"), "col")
    return jax.shard_map(
        on_device, mesh=mesh, in_specs=in_specs, out_specs=out_specs, check_vma=False
    )
```

profile of v0, /device:TPU:0, one launch (start us, length us, event | category | flops | bytes accessed | tf_op | source)
XLA Modules:
  0.0 149.5 jit_solution(4870484490254769119)
XLA Ops:
  1.0 5.0 %collective-permute-start = (bf16[2,8,16,2]{3,2,1,0:T(8,128)(2,1)S(1)}, bf16[2,8,16,2]{3,2,1,0:T(8,128)(2,1)S(1)}, u32[]{:S(2)}, u32[]{:S(2)}) collective-permute-start(bf16[2,8,16,2]{3,2,1,0:T(8,128)(2,1)S(1)} %get-tuple-element.302), channel_id=1, source_target_pairs={{0,4},{4,8},{8,12},{1,5},{5,9},{9,13},{2,6},{6,10},{10,14},{3,7},{... | collective-permute-start | bytes 3080 | tf_op jit(solution)/shard_map/ppermute | solution.py:17
  7.9 4.3 %collective-permute-done.1 = bf16[2,8,16,2]{3,2,1,0:T(8,128)(2,1)S(1)} collective-permute-done((bf16[2,8,16,2]{3,2,1,0:T(8,128)(2,1)S(1)}, bf16[2,8,16,2]{3,2,1,0:T(8,128)(2,1)S(1)}, u32[]{:S(2)}, u32[]{:S(2)}) %collective-permute-start.1) | collective-permute-done | bytes 1056 | tf_op jit(solution)/shard_map/ppermute | solution.py:18
  15.0 3.4 %collective-permute-done.3 = bf16[2,8,2,132]{3,2,1,0:T(2,128)(2,1)S(1)} collective-permute-done((bf16[2,8,2,132]{3,2,1,0:T(2,128)(2,1)S(1)}, bf16[2,8,2,132]{3,2,1,0:T(2,128)(2,1)S(1)}, u32[]{:S(2)}, u32[]{:S(2)}) %collective-permute-start.3) | collective-permute-done | bytes 8480 | tf_op jit(solution)/shard_map/ppermute | solution.py:18
  23.4 3.5 %collective-permute-start.4 = (bf16[32,18,64]{2,1,0:T(8,128)(2,1)S(1)}, bf16[32,18,64]{2,1,0:T(8,128)(2,1)S(1)}, u32[]{:S(2)}, u32[]{:S(2)}) collective-permute-start(bf16[32,18,64]{2,1,0:T(8,128)(2,1)S(1)} %slice.589), channel_id=1, source_target_pairs={{0,4},{4,8},{8,12},{1,5},{5,9},{9,13},{2,6},{6,10},{10,14},{3,7},{... | collective-permute-start | bytes 221192 | tf_op jit(solution)/shard_map/ppermute | solution.py:26
  27.0 3.6 %collective-permute-done.4 = bf16[32,18,64]{2,1,0:T(8,128)(2,1)S(1)} collective-permute-done((bf16[32,18,64]{2,1,0:T(8,128)(2,1)S(1)}, bf16[32,18,64]{2,1,0:T(8,128)(2,1)S(1)}, u32[]{:S(2)}, u32[]{:S(2)}) %collective-permute-start.4) | collective-permute-done | bytes 73760 | tf_op jit(solution)/shard_map/ppermute | solution.py:26
  30.9 118.0 %while.19 = (s32[]{:T(128)}, f32[16,128]{1,0:T(8,128)S(1)}, f32[16,128]{1,0:T(8,128)S(1)}, f32[16,128]{1,0:T(8,128)S(1)}, s32[4]{0:T(128)S(1)}, /*index=5*/bf16[...) while((s32[]{:T(128)}, f32[16,128]{1,0:T(8,128)S(1)}, ...), condition=%wide.region_4.5_spmd.clone, body=%wide.region_0.4_spmd.clone.sunk | while | flops 114660688 | bytes 30197976 | solution.py:145
  32.4 4.1 %constant_dynamic-slice_fusion.19 = (bf16[32,18,130]{2,1,0:T(8,128)(2,1)S(1)}, bf16[32,18,130]{2,1,0:T(8,128)(2,1)S(1)}, bf16[32,18,130]{2,1,0:T(8,128)(2,1)S(1)...) fusion(bf16[32,18,195]{2,1,0:T(8,128)(2,1)S(1)} %get-tuple-elem, ...), kind=kLoop, calls=%fused_computation.144.clone.1 | loop fusion | bytes 5391432 | tf_op jit(solution)/shard_map/while/body/eval_jaxpr/slice | solution.py:64
  36.5 3.8 %fusion.124 = (f32[8,18,130]{2,1,0:T(8,128)S(1)}, f32[8,18,130]{2,1,0:T(8,128)S(1)}, f32[8,18,130]{2,1,0:T(8,128)S(1)}, f32[8,18,130]{2,1,0:T(8,128)S(1)}, f32[8...) fusion(bf16[32,18,130]{2,1,0:T(8,128)(2,1)S(1)} %get-tuple-elem, ...), kind=kLoop, calls=%fused_computation.36.clone.1 | loop fusion | flops 3781440 | bytes 4193280 | tf_op jit(solution)/shard_map/while
  49.8 4.3 %convolution_bitcast_fusion.2 = f32[27,18,18,130]{3,0,2,1:T(8,128)S(1)} fusion(bf16[8,18,18,130]{3,0,2,1:T(8,128)(2,1)S(1)} %fusion.142, f32[8,27]{1,0:T(8,128)S(1)} %get-tuple-element.600), kind=kOutput, calls=%fused_computation.18.clone.1 | convolution fusion | flops 109175040 | bytes 5223744 | tf_op jit(solution)/shard_map/while/body/eval_jaxpr/gdyx,gk->kdyx/dot_general | solution.py:78
  54.1 4.4 %fusion.144 = (f32[1,16,16,128]{3,0,2,1:T(1,128)S(1)}, f32[1,16,16,128]{3,0,2,1:T(1,128)S(1)}, f32[1,16,16,128]{3,0,2,1:T(1,128)S(1)}, f32[1,16,16,128]{3,0,2,1:...) fusion(f32[27,18,18,130]{3,0,2,1:T(8,128)S(1)} %convolution_bit, ...), kind=kLoop, calls=%fused_computation.186.clone.1 | loop fusion | bytes 4980736 | tf_op jit(solution)/shard_map/while/body/eval_jaxpr/slice | solution.py:87
  61.8 4.1 %constant_dynamic-slice_fusion.19 = (bf16[32,18,130]{2,1,0:T(8,128)(2,1)S(1)}, bf16[32,18,130]{2,1,0:T(8,128)(2,1)S(1)}, bf16[32,18,130]{2,1,0:T(8,128)(2,1)S(1)...) fusion(bf16[32,18,195]{2,1,0:T(8,128)(2,1)S(1)} %get-tuple-elem, ...), kind=kLoop, calls=%fused_computation.144.clone.1 | loop fusion | bytes 5391432 | tf_op jit(solution)/shard_map/while/body/eval_jaxpr/slice | solution.py:64
  65.9 3.8 %fusion.124 = (f32[8,18,130]{2,1,0:T(8,128)S(1)}, f32[8,18,130]{2,1,0:T(8,128)S(1)}, f32[8,18,130]{2,1,0:T(8,128)S(1)}, f32[8,18,130]{2,1,0:T(8,128)S(1)}, f32[8...) fusion(bf16[32,18,130]{2,1,0:T(8,128)(2,1)S(1)} %get-tuple-elem, ...), kind=kLoop, calls=%fused_computation.36.clone.1 | loop fusion | flops 3781440 | bytes 4193280 | tf_op jit(solution)/shard_map/while
  79.2 4.3 %convolution_bitcast_fusion.2 = f32[27,18,18,130]{3,0,2,1:T(8,128)S(1)} fusion(bf16[8,18,18,130]{3,0,2,1:T(8,128)(2,1)S(1)} %fusion.142, f32[8,27]{1,0:T(8,128)S(1)} %get-tuple-element.600), kind=kOutput, calls=%fused_computation.18.clone.1 | convolution fusion | flops 109175040 | bytes 5223744 | tf_op jit(solution)/shard_map/while/body/eval_jaxpr/gdyx,gk->kdyx/dot_general | solution.py:78
  83.6 4.4 %fusion.144 = (f32[1,16,16,128]{3,0,2,1:T(1,128)S(1)}, f32[1,16,16,128]{3,0,2,1:T(1,128)S(1)}, f32[1,16,16,128]{3,0,2,1:T(1,128)S(1)}, f32[1,16,16,128]{3,0,2,1:...) fusion(f32[27,18,18,130]{3,0,2,1:T(8,128)S(1)} %convolution_bit, ...), kind=kLoop, calls=%fused_computation.186.clone.1 | loop fusion | bytes 4980736 | tf_op jit(solution)/shard_map/while/body/eval_jaxpr/slice | solution.py:87
  88.0 1.6 %fusion.143 = (f32[1,16,16,128]{3,0,2,1:T(1,128)S(1)}, f32[1,16,16,128]{3,0,2,1:T(1,128)S(1)}, f32[1,16,16,128]{3,0,2,1:T(1,128)S(1)}, f32[1,16,16,128]{3,0,2,1:...) fusion(f32[27,18,18,130]{3,0,2,1:T(8,128)S(1)} %convolution_bit, ...), kind=kLoop, calls=%fused_computation.187.clone.1 | loop fusion | bytes 2097152 | tf_op jit(solution)/shard_map/while/body/eval_jaxpr/slice | solution.py:87
  91.3 4.1 %constant_dynamic-slice_fusion.19 = (bf16[32,18,130]{2,1,0:T(8,128)(2,1)S(1)}, bf16[32,18,130]{2,1,0:T(8,128)(2,1)S(1)}, bf16[32,18,130]{2,1,0:T(8,128)(2,1)S(1)...) fusion(bf16[32,18,195]{2,1,0:T(8,128)(2,1)S(1)} %get-tuple-elem, ...), kind=kLoop, calls=%fused_computation.144.clone.1 | loop fusion | bytes 5391432 | tf_op jit(solution)/shard_map/while/body/eval_jaxpr/slice | solution.py:64
  95.4 3.8 %fusion.124 = (f32[8,18,130]{2,1,0:T(8,128)S(1)}, f32[8,18,130]{2,1,0:T(8,128)S(1)}, f32[8,18,130]{2,1,0:T(8,128)S(1)}, f32[8,18,130]{2,1,0:T(8,128)S(1)}, f32[8...) fusion(bf16[32,18,130]{2,1,0:T(8,128)(2,1)S(1)} %get-tuple-elem, ...), kind=kLoop, calls=%fused_computation.36.clone.1 | loop fusion | flops 3781440 | bytes 4193280 | tf_op jit(solution)/shard_map/while
  108.7 4.3 %convolution_bitcast_fusion.2 = f32[27,18,18,130]{3,0,2,1:T(8,128)S(1)} fusion(bf16[8,18,18,130]{3,0,2,1:T(8,128)(2,1)S(1)} %fusion.142, f32[8,27]{1,0:T(8,128)S(1)} %get-tuple-element.600), kind=kOutput, calls=%fused_computation.18.clone.1 | convolution fusion | flops 109175040 | bytes 5223744 | tf_op jit(solution)/shard_map/while/body/eval_jaxpr/gdyx,gk->kdyx/dot_general | solution.py:78
  113.0 4.4 %fusion.144 = (f32[1,16,16,128]{3,0,2,1:T(1,128)S(1)}, f32[1,16,16,128]{3,0,2,1:T(1,128)S(1)}, f32[1,16,16,128]{3,0,2,1:T(1,128)S(1)}, f32[1,16,16,128]{3,0,2,1:...) fusion(f32[27,18,18,130]{3,0,2,1:T(8,128)S(1)} %convolution_bit, ...), kind=kLoop, calls=%fused_computation.186.clone.1 | loop fusion | bytes 4980736 | tf_op jit(solution)/shard_map/while/body/eval_jaxpr/slice | solution.py:87
  117.4 1.6 %fusion.143 = (f32[1,16,16,128]{3,0,2,1:T(1,128)S(1)}, f32[1,16,16,128]{3,0,2,1:T(1,128)S(1)}, f32[1,16,16,128]{3,0,2,1:T(1,128)S(1)}, f32[1,16,16,128]{3,0,2,1:...) fusion(f32[27,18,18,130]{3,0,2,1:T(8,128)S(1)} %convolution_bit, ...), kind=kLoop, calls=%fused_computation.187.clone.1 | loop fusion | bytes 2097152 | tf_op jit(solution)/shard_map/while/body/eval_jaxpr/slice | solution.py:87
  120.8 4.1 %constant_dynamic-slice_fusion.19 = (bf16[32,18,130]{2,1,0:T(8,128)(2,1)S(1)}, bf16[32,18,130]{2,1,0:T(8,128)(2,1)S(1)}, bf16[32,18,130]{2,1,0:T(8,128)(2,1)S(1)...) fusion(bf16[32,18,195]{2,1,0:T(8,128)(2,1)S(1)} %get-tuple-elem, ...), kind=kLoop, calls=%fused_computation.144.clone.1 | loop fusion | bytes 5391432 | tf_op jit(solution)/shard_map/while/body/eval_jaxpr/slice | solution.py:64
  124.8 3.8 %fusion.124 = (f32[8,18,130]{2,1,0:T(8,128)S(1)}, f32[8,18,130]{2,1,0:T(8,128)S(1)}, f32[8,18,130]{2,1,0:T(8,128)S(1)}, f32[8,18,130]{2,1,0:T(8,128)S(1)}, f32[8...) fusion(bf16[32,18,130]{2,1,0:T(8,128)(2,1)S(1)} %get-tuple-elem, ...), kind=kLoop, calls=%fused_computation.36.clone.1 | loop fusion | flops 3781440 | bytes 4193280 | tf_op jit(solution)/shard_map/while
  138.1 4.3 %convolution_bitcast_fusion.2 = f32[27,18,18,130]{3,0,2,1:T(8,128)S(1)} fusion(bf16[8,18,18,130]{3,0,2,1:T(8,128)(2,1)S(1)} %fusion.142, f32[8,27]{1,0:T(8,128)S(1)} %get-tuple-element.600), kind=kOutput, calls=%fused_computation.18.clone.1 | convolution fusion | flops 109175040 | bytes 5223744 | tf_op jit(solution)/shard_map/while/body/eval_jaxpr/gdyx,gk->kdyx/dot_general | solution.py:78
  142.5 4.4 %fusion.144 = (f32[1,16,16,128]{3,0,2,1:T(1,128)S(1)}, f32[1,16,16,128]{3,0,2,1:T(1,128)S(1)}, f32[1,16,16,128]{3,0,2,1:T(1,128)S(1)}, f32[1,16,16,128]{3,0,2,1:...) fusion(f32[27,18,18,130]{3,0,2,1:T(8,128)S(1)} %convolution_bit, ...), kind=kLoop, calls=%fused_computation.186.clone.1 | loop fusion | bytes 4980736 | tf_op jit(solution)/shard_map/while/body/eval_jaxpr/slice | solution.py:87
  (161 shorter events, 55.5 us)
Async XLA Ops:
  0.0 20.6 %copy-start = (bf16[32,72]{1,0:T(8,128)(2,1)S(1)}, bf16[32,72]{1,0:T(8,128)(2,1)}, u32[]{:S(2)}) copy-start(bf16[32,72]{1,0:T(8,128)(2,1)} %param.7) | copy-start | bytes 13828
  1.0 6.9 %collective-permute-start = (bf16[2,8,16,2]{3,2,1,0:T(8,128)(2,1)S(1)}, bf16[2,8,16,2]{3,2,1,0:T(8,128)(2,1)S(1)}, u32[]{:S(2)}, u32[]{:S(2)}) collective-permute-start(bf16[2,8,16,2]{3,2,1,0:T(8,128)(2,1)S(1)} %get-tuple-element.302), channel_id=1, source_target_pairs={{0,4},{4,8},{8,12},{1,5},{5,9},{9,13},{2,6},{6,10},{10,14},{3,7},{... | collective-permute-start | bytes 3080 | tf_op jit(solution)/shard_map/ppermute | solution.py:17
  6.0 6.2 %collective-permute-start.1 = (bf16[2,8,16,2]{3,2,1,0:T(8,128)(2,1)S(1)}, bf16[2,8,16,2]{3,2,1,0:T(8,128)(2,1)S(1)}, u32[]{:S(2)}, u32[]{:S(2)}) collective-permute-start(bf16[2,8,16,2]{3,2,1,0:T(8,128)(2,1)S(1)} %get-tuple-element.303), channel_id=1, source_target_pairs={{4,0},{8,4},{12,8},{5,1},{9,5},{13,9},{6,2},{10,6},{14,10},{7,3},{... | collective-permute-start | bytes 3080 | tf_op jit(solution)/shard_map/ppermute | solution.py:18
  12.3 2.7 %collective-permute-start.2 = (bf16[2,8,2,132]{3,2,1,0:T(2,128)(2,1)S(1)}, bf16[2,8,2,132]{3,2,1,0:T(2,128)(2,1)S(1)}, u32[]{:S(2)}, u32[]{:S(2)}) collective-permute-start(bf16[2,8,2,132]{3,2,1,0:T(2,128)(2,1)S(1)} %get-tuple-element.300), channel_id=1, source_target_pairs={{0,1},{1,2},{2,3},{4,5},{5,6},{6,7},{8,9},{9,10},{10,11},{12,13},{... | collective-permute-start | bytes 25352 | tf_op jit(solution)/shard_map/ppermute | solution.py:17
  13.6 4.8 %collective-permute-start.3 = (bf16[2,8,2,132]{3,2,1,0:T(2,128)(2,1)S(1)}, bf16[2,8,2,132]{3,2,1,0:T(2,128)(2,1)S(1)}, u32[]{:S(2)}, u32[]{:S(2)}) collective-permute-start(bf16[2,8,2,132]{3,2,1,0:T(2,128)(2,1)S(1)} %get-tuple-element.301), channel_id=1, source_target_pairs={{1,0},{2,1},{3,2},{5,4},{6,5},{7,6},{9,8},{10,9},{11,10},{13,12},{... | collective-permute-start | bytes 25352 | tf_op jit(solution)/shard_map/ppermute | solution.py:18
  19.4 1.2 copy-start.3
  22.4 8.5 %copy-start.2 = (f32[8,27]{1,0:T(8,128)S(1)}, f32[8,27]{1,0:T(8,128)}, u32[]{:S(2)}) copy-start(f32[8,27]{1,0:T(8,128)} %param.9) | copy-start | bytes 2596
  23.4 7.3 %collective-permute-start.4 = (bf16[32,18,64]{2,1,0:T(8,128)(2,1)S(1)}, bf16[32,18,64]{2,1,0:T(8,128)(2,1)S(1)}, u32[]{:S(2)}, u32[]{:S(2)}) collective-permute-start(bf16[32,18,64]{2,1,0:T(8,128)(2,1)S(1)} %slice.589), channel_id=1, source_target_pairs={{0,4},{4,8},{8,12},{1,5},{5,9},{9,13},{2,6},{6,10},{10,14},{3,7},{... | collective-permute-start | bytes 221192 | tf_op jit(solution)/shard_map/ppermute | solution.py:26
  32.4 4.1 %copy-start.1 = (bf16[32,18,130]{2,1,0:T(8,128)(2,1)S(1)}, bf16[32,18,130]{2,1,0:T(8,128)(2,1)}, u32[]{:S(2)}) copy-start(bf16[32,18,130]{2,1,0:T(8,128)(2,1)} %get-tuple-element.599) | copy-start | bytes 449284 | tf_op jit(solution)/shard_map/while
  61.8 4.1 %copy-start.1 = (bf16[32,18,130]{2,1,0:T(8,128)(2,1)S(1)}, bf16[32,18,130]{2,1,0:T(8,128)(2,1)}, u32[]{:S(2)}) copy-start(bf16[32,18,130]{2,1,0:T(8,128)(2,1)} %get-tuple-element.599) | copy-start | bytes 449284 | tf_op jit(solution)/shard_map/while
  91.3 4.1 %copy-start.1 = (bf16[32,18,130]{2,1,0:T(8,128)(2,1)S(1)}, bf16[32,18,130]{2,1,0:T(8,128)(2,1)}, u32[]{:S(2)}) copy-start(bf16[32,18,130]{2,1,0:T(8,128)(2,1)} %get-tuple-element.599) | copy-start | bytes 449284 | tf_op jit(solution)/shard_map/while
  120.8 4.1 %copy-start.1 = (bf16[32,18,130]{2,1,0:T(8,128)(2,1)S(1)}, bf16[32,18,130]{2,1,0:T(8,128)(2,1)}, u32[]{:S(2)}) copy-start(bf16[32,18,130]{2,1,0:T(8,128)(2,1)} %get-tuple-element.599) | copy-start | bytes 449284 | tf_op jit(solution)/shard_map/while
where the time goes:
time: 152 us; the launch traced here: 150 us
  other arithmetic  56.7 us (37%)
  local copies, waits for them, and re-layouts  46.3 us (30%)
  matrix products  17.7 us (12%)
  starting transfers between devices  12.3 us (8%)
  waiting for transfers between devices  11.9 us (8%)
  loops' own time  4.22 us (3%)
    while x72, other arithmetic  51.9 us
    slice x8, local copies, waits for them, and re-layouts, aggregate(): tapped[9 * step_d + 3 * step_y + step_x, step_d:step_d + block_depth, ste...  23.9 us
    dot_general x4, matrix products, aggregate(): jnp.einsum('gdyx,gk->kdyx', cost_block.astype(jnp.float32), agg_weight, p...  17.4 us
    slice x4, local copies, waits for them, and re-layouts, block_costs(): window[:, :, block_depth + 1 - offset:block_depth + 1 - offset + width_out]  16.3 us
    ppermute x2, waiting for transfers between devices, with_halo(): after = lax.ppermute(leading, axis, down)  7.7 us
    ppermute x2, starting transfers between devices, with_halo(): before = lax.ppermute(last, axis, up)  6.25 us
    another operation x1, loops' own time, on_device(): lax.scan(advance, initial, jnp.arange(D // DB, dtype=jnp.int32))  4.22 us
    ppermute x1, waiting for transfers between devices, from_behind(): return lax.ppermute(shard, axis, pairs)  3.65 us
  transfers between devices with their start and end apart: 5, of which 4 were waited for; matrix products, arithmetic and copies ran while one was open for 0% of the time, Pallas kernels for 0%

commit v1 on v0

v1 whole, which is shorter than its diff:
```python
import functools

import jax
import jax.numpy as jnp
from jax import lax
from jax.experimental import pallas as pl
from jax.experimental.pallas import tpu as pltpu
from jax.sharding import PartitionSpec as P

D = 64
BAND = 4


def shifted(shard, axes, sizes, steps):
    pairs = []
    for r in range(sizes[1]):
        for c in range(sizes[0]):
            to_r, to_c = r - steps[0], c - steps[1]
            if 0 <= to_r < sizes[1] and 0 <= to_c < sizes[0]:
                pairs.append((c * sizes[1] + r, to_c * sizes[1] + to_r))
    return lax.ppermute(shard, axes, pairs)


def body(shape, pt_ref, q_ref, bias_ref, agg_ref, out_ref, wc, amat, lf, rf, cost, acc, score):
    rows, cols, groups, per, cin = shape
    lanes = wc.shape[2] // per
    lead = D + 8
    span = rf.shape[1]
    tiles = lanes // 128
    total_rows = rows * lax.axis_size("row")
    total_cols = cols * lax.axis_size("col")
    top = lax.axis_index("row") * rows - 1
    left = lax.axis_index("col") * cols

    lane_row = lax.broadcasted_iota(jnp.int32, (cin, lanes), 1) // groups
    for step_x in range(3):
        for ch in range(per):
            taps = []
            for step_y in range(3):
                base = ((step_y * 3 + step_x) * per + ch) * cin
                taps.append(q_ref[base : base + cin, :])
            for pair in range((rows + 4) // 2):
                halves = []
                for line in (2 * pair, 2 * pair + 1):
                    value = jnp.zeros((cin, lanes), jnp.float32)
                    for step_y in range(3):
                        value = jnp.where(lane_row == line - step_y, taps[step_y], value)
                    halves.append(value)
                wc[step_x, pair * 2 * cin : (pair + 1) * 2 * cin, ch * lanes : (ch + 1) * lanes] = (
                    jnp.concatenate(halves, axis=0).astype(jnp.bfloat16)
                )
    used = (rows + 4) * cin
    if used < lanes:
        wc[:, used:, :] = jnp.zeros((3, lanes - used, per * lanes), jnp.bfloat16)

    off = (
        lax.broadcasted_iota(jnp.int32, (rows, lanes), 1) // groups
        - lax.broadcasted_iota(jnp.int32, (rows, lanes), 0)
    )
    for step_d in range(3):
        for step_x in range(3):
            value = jnp.zeros((rows, lanes), jnp.float32)
            for step_y in range(3):
                k = 9 * step_d + 3 * step_y + step_x
                value = jnp.where(off == step_y, agg_ref[k : k + 1, :], value)
            high = value.astype(jnp.bfloat16)
            low = (value - high.astype(jnp.float32)).astype(jnp.bfloat16)
            at = (step_d * 3 + step_x) * 2 * rows
            amat[at : at + rows, :] = high
            amat[at + rows : at + 2 * rows, :] = low

    def features(image, first, count, store, scale):
        row_ids = left + first - lead + lax.broadcasted_iota(jnp.int32, (count, lanes), 0)
        line = top + lax.broadcasted_iota(jnp.int32, (count, lanes), 1) // groups
        keep = (row_ids >= 0) & (row_ids < total_cols) & (line >= 0) & (line < total_rows)
        parts = [
            pt_ref[image, 7 + step_x + first : 7 + step_x + first + count, :].astype(jnp.bfloat16)
            for step_x in range(3)
        ]
        for ch in range(per):
            summed = jnp.broadcast_to(bias_ref[ch : ch + 1, :], (count, lanes))
            total = None
            for step_x in range(3):
                term = jnp.dot(
                    parts[step_x],
                    wc[step_x, :, ch * lanes : (ch + 1) * lanes],
                    preferred_element_type=jnp.float32,
                )
                total = term if total is None else total + term
            summed = total + summed
            feat = jnp.where(summed >= 0, summed, summed * 0.1)
            feat = feat.astype(jnp.bfloat16).astype(jnp.float32)
            feat = jnp.where(keep, feat * scale, 0.0)
            for tile in range(tiles):
                store[ch * tiles + tile, :, :] = feat[:, tile * 128 : (tile + 1) * 128]

    features(0, lead - 8, cols + 16, lf, 1.0 / per)
    features(1, 0, span, rf, 1.0)

    for tile in range(tiles):
        for chunk in range(cols // 16):
            lefts = [
                lf[ch * tiles + tile, 8 + chunk * 16 : 24 + chunk * 16, :] for ch in range(per)
            ]

            def layer(d, carry):
                total = None
                for ch in range(per):
                    term = (
                        lefts[ch] * rf[ch * tiles + tile, pl.ds(lead + chunk * 16 - d, 16), :]
                    )
                    total = term if total is None else total + term
                cost[d, chunk * 16 : (chunk + 1) * 16, tile * 128 : (tile + 1) * 128] = (
                    total.astype(jnp.bfloat16)
                )
                return carry

            lax.fori_loop(0, D, layer, 0, unroll=4)

    edges = []
    for at, begin in ((7, lead - D), (8 + cols, lead + cols - D + 1)):
        parts = []
        for tile in range(tiles):
            total = None
            for ch in range(per):
                k = ch * tiles + tile
                term = lf[k, at : at + 1, :] * rf[k, begin : begin + D, :]
                total = term if total is None else total + term
            parts.append(total.astype(jnp.bfloat16))
        edges.append(jnp.concatenate(parts, axis=1))
    edge = jnp.concatenate(edges, axis=0)
    nt = (((1,), (1,)), ((), ()))
    side = lax.dot_general(amat[...], edge, nt, preferred_element_type=jnp.float32)
    place = lax.broadcasted_iota(jnp.int32, (rows, 2 * D), 1)
    within = jnp.where(place >= D, place - D, place)
    border = None
    for step_d in range(3):
        pick = []
        for step_x in (0, 2):
            at = (step_d * 3 + step_x) * 2 * rows
            pick.append(side[at : at + rows, :] + side[at + rows : at + 2 * rows, :])
        value = jnp.where(place < D, pick[0], pick[1])
        if step_d == 0:
            value = jnp.where(within == D - 1, 0.0, pltpu.roll(value, 2 * D - 1, 1))
        elif step_d == 2:
            value = jnp.where(within == 0, 0.0, pltpu.roll(value, 1, 1))
        border = value if border is None else border + value

    acc[...] = jnp.zeros_like(acc)

    def band(block, carry):
        d0 = block * BAND
        stack = cost[pl.ds(d0, BAND), :, :].reshape(BAND * cols, lanes)
        got = lax.dot_general(amat[...], stack, nt, preferred_element_type=jnp.float32)
        for step_x in range(3):
            for o in range(BAND + 2):
                value = acc[step_x, d0 + o, :, :]
                for step_d in range(3):
                    j = o + step_d - 2
                    if 0 <= j < BAND:
                        at = (step_d * 3 + step_x) * 2 * rows
                        value += got[at : at + rows, j * cols : (j + 1) * cols]
                        value += got[at + rows : at + 2 * rows, j * cols : (j + 1) * cols]
                acc[step_x, d0 + o, :, :] = value
        return carry

    lax.fori_loop(0, D // BAND, band, 0)

    lane = lax.broadcasted_iota(jnp.int32, (rows, cols), 1)

    def finish(d, best):
        before = jnp.where(
            lane == 0,
            pltpu.roll(border, lax.rem(d + D + 1, 2 * D), 1),
            pltpu.roll(acc[0, d + 1, :, :], 1, 1),
        )
        after = jnp.where(
            lane == cols - 1, pltpu.roll(border, d, 1), pltpu.roll(acc[2, d + 1, :, :], cols - 1, 1)
        )
        value = acc[1, d + 1, :, :] + before + after
        score[d, :, :] = value
        return jnp.maximum(best, value)

    best = lax.fori_loop(0, D, finish, jnp.full((rows, cols), -jnp.inf, jnp.float32), unroll=4)

    def weigh(d, carry):
        total, moment = carry
        weight = jnp.exp(score[d, :, :] - best)
        return total + weight, moment + weight * d.astype(jnp.float32)

    zero = jnp.zeros((rows, cols), jnp.float32)
    total, moment = lax.fori_loop(0, D, weigh, (zero, zero), unroll=4)
    out_ref[...] = moment / total / D


def on_device(images, conv_weight, conv_bias, agg_weight):
    cin, rows, cols = images.shape[1:]
    groups = agg_weight.shape[0]
    per = conv_weight.shape[0] // groups
    lanes = -(-max((rows + 2) * groups, (rows + 4) * cin) // 128) * 128
    span = cols + D + 16
    sizes = (lax.axis_size("col"), lax.axis_size("row"))
    pictures = images.astype(jnp.bfloat16)
    move = functools.partial(shifted, axes=("col", "row"), sizes=sizes)
    wide = D + 2
    grid = []
    for r, lines in ((-1, slice(rows - 2, rows)), (0, slice(0, rows)), (1, slice(0, 2))):
        line = []
        for c, columns in ((-1, slice(cols - wide, cols)), (0, slice(0, cols)), (1, slice(0, 2))):
            piece = pictures[:, :, lines, columns]
            line.append(piece if r == 0 and c == 0 else move(piece, steps=(r, c)))
        grid.append(jnp.concatenate(line, axis=3))
    ext = jnp.concatenate(grid, axis=2)
    pt = ext.transpose(0, 3, 2, 1).reshape(2, ext.shape[3], (rows + 4) * cin).astype(jnp.float32)
    ahead = 16 + D - wide
    pt = jnp.pad(
        pt, ((0, 0), (ahead, span + 16 - ahead - pt.shape[1]), (0, lanes - pt.shape[2]))
    )
    repeat = lanes // groups
    q = conv_weight.reshape(groups, per, 9, cin).transpose(2, 1, 3, 0).astype(jnp.float32)
    q = jnp.tile(q.reshape(9 * per * cin, groups), (1, repeat))
    bias = jnp.tile(conv_bias.reshape(groups, per).T, (1, repeat))
    agg = jnp.tile(agg_weight.T, (1, repeat))
    return pl.pallas_call(
        functools.partial(body, (rows, cols, groups, per, cin)),
        out_shape=jax.ShapeDtypeStruct((rows, cols), jnp.float32),
        in_specs=[pl.BlockSpec(memory_space=pltpu.VMEM)] * 4,
        out_specs=pl.BlockSpec(memory_space=pltpu.VMEM),
        scratch_shapes=[
            pltpu.VMEM((3, lanes, per * lanes), jnp.bfloat16),
            pltpu.VMEM((18 * rows, lanes), jnp.bfloat16),
            pltpu.VMEM((per * (lanes // 128), cols + 16, 128), jnp.float32),
            pltpu.VMEM((per * (lanes // 128), span, 128), jnp.float32),
            pltpu.VMEM((D, cols, lanes), jnp.bfloat16),
            pltpu.VMEM((3, D + 2, rows, cols), jnp.float32),
            pltpu.VMEM((D, rows, cols), jnp.float32),
        ],
    )(pt, q, bias, agg)


def solution(mesh):
    in_specs = (P("pairs", None, "row", "col"), P(), P(), P())
    out_specs = P(("pairs", "row"), "col")
    return jax.shard_map(
        on_device, mesh=mesh, in_specs=in_specs, out_specs=out_specs, check_vma=False
    )
```

time: 152 us -> 40.5 us (0.27)
  the two profiles are of different devices: /device:TPU:0 before, /device:TPU:18 now
where the time goes in v1:
time: 40.5 us; the launch traced here: 40.1 us
  starting transfers between devices  19.8 us (49%)
  Pallas kernels  13.1 us (32%)
  local copies, waits for them, and re-layouts  4.04 us (10%)
  waiting for transfers between devices  1.99 us (5%)
  other arithmetic  0.96 us (2%)
    ppermute x8, starting transfers between devices, shifted(): return lax.ppermute(shard, axes, pairs)  19.8 us
    pallas_call x1, Pallas kernels, on_device(): pl.pallas_call(functools.partial(body, (rows, cols, groups, per, cin)), o...  13.1 us
    ppermute x8, waiting for transfers between devices, shifted(): return lax.ppermute(shard, axes, pairs)  1.99 us
    another operation x5, local copies, waits for them, and re-layouts, on_device(): q = jnp.tile(q.reshape(9 * per * cin, groups), (1, repeat))  1.18 us
    unnamed x7, local copies, waits for them, and re-layouts  0.98 us
    pad x1, other arithmetic, on_device(): jnp.pad(pt, ((0, 0), (ahead, span + 16 - ahead - pt.shape[1]), (0, lanes...  0.83 us
  transfers between devices with their start and end apart: 8, of which 1 were waited for; matrix products, arithmetic and copies ran while one was open for 7% of the time, Pallas kernels for 0%

profile of v1, /device:TPU:18, one launch (start us, length us, event | category | flops | bytes accessed | tf_op | source)
XLA Modules:
  0.0 40.1 jit_solution(17782094498516376457)
XLA Ops:
  0.0 1.0 %copy.15 = bf16[2,8,16,128]{3,1,2,0:T(8,128)(2,1)S(1)} copy(f32[2,8,16,128]{3,2,1,0:T(8,128)} %param.4) | data formatting | bytes 196608 | tf_op args[0]
  1.0 0.1 fusion
  1.0 2.9 %collective-permute-start = (bf16[2,8,2,66]{3,1,2,0:T(8,128)(2,1)S(1)}, bf16[2,8,2,66]{3,1,2,0:T(8,128)(2,1)S(1)}, u32[]{:S(2)}, u32[]{:S(2)}) collective-permute-start(bf16[2,8,2,66]{3,1,2,0:T(8,128)(2,1)S(1)} %get-tuple-element.5), channel_id=1, source_target_pairs={{0,5},{4,9},{8,13},{1,6},{5,10},{9,14},{2,7},{6,11},{10,15},{16,21... | collective-permute-start | bytes 12680 | tf_op jit(solution)/shard_map/ppermute | solution.py:21
  4.0 1.9 %collective-permute-start.1 = (bf16[2,8,2,128]{3,1,2,0:T(8,128)(2,1)S(1)}, bf16[2,8,2,128]{3,1,2,0:T(8,128)(2,1)S(1)}, u32[]{:S(2)}, u32[]{:S(2)}) collective-permute-start(bf16[2,8,2,128]{3,1,2,0:T(8,128)(2,1)S(1)} %get-tuple-element.7), channel_id=1, source_target_pairs={{0,1},{4,5},{8,9},{12,13},{1,2},{5,6},{9,10},{13,14},{2,3},{6,7},{... | collective-permute-start | bytes 24584 | tf_op jit(solution)/shard_map/ppermute | solution.py:21
  5.9 1.9 %collective-permute-start.2 = (bf16[2,8,2,2]{3,1,2,0:T(8,128)(2,1)S(1)}, bf16[2,8,2,2]{3,1,2,0:T(8,128)(2,1)S(1)}, u32[]{:S(2)}, u32[]{:S(2)}) collective-permute-start(bf16[2,8,2,2]{3,1,2,0:T(8,128)(2,1)S(1)} %get-tuple-element.9), channel_id=1, source_target_pairs={{4,1},{8,5},{12,9},{5,2},{9,6},{13,10},{6,3},{10,7},{14,11},{20,17... | collective-permute-start | bytes 392 | tf_op jit(solution)/shard_map/ppermute | solution.py:21
  7.9 3.5 %collective-permute-start.7 = (bf16[2,8,2,2]{3,1,2,0:T(8,128)(2,1)S(1)}, bf16[2,8,2,2]{3,1,2,0:T(8,128)(2,1)S(1)}, u32[]{:S(2)}, u32[]{:S(2)}) collective-permute-start(bf16[2,8,2,2]{3,1,2,0:T(8,128)(2,1)S(1)} %get-tuple-element.10), channel_id=1, source_target_pairs={{5,0},{9,4},{13,8},{6,1},{10,5},{14,9},{7,2},{11,6},{15,10},{21,16... | collective-permute-start | bytes 392 | tf_op jit(solution)/shard_map/ppermute | solution.py:21
  11.4 1.9 %collective-permute-start.4 = (bf16[2,8,16,2]{3,1,2,0:T(8,128)(2,1)S(1)}, bf16[2,8,16,2]{3,1,2,0:T(8,128)(2,1)S(1)}, u32[]{:S(2)}, u32[]{:S(2)}) collective-permute-start(bf16[2,8,16,2]{3,1,2,0:T(8,128)(2,1)S(1)} %bitcast.16), channel_id=1, source_target_pairs={{4,0},{8,4},{12,8},{5,1},{9,5},{13,9},{6,2},{10,6},{14,10},{7,3},{... | collective-permute-start | bytes 3080 | tf_op jit(solution)/shard_map/ppermute | solution.py:21
  13.3 0.1 reshape.24
  13.5 0.1 copy.10
  13.5 0.1 reshape.23
  13.7 0.1 slice.35
  13.8 3.8 %collective-permute-start.5 = (bf16[2,8,2,66]{3,1,2,0:T(8,128)(2,1)S(1)}, bf16[2,8,2,66]{3,1,2,0:T(8,128)(2,1)S(1)}, u32[]{:S(2)}, u32[]{:S(2)}) collective-permute-start(bf16[2,8,2,66]{3,1,2,0:T(8,128)(2,1)S(1)} %get-tuple-element.6), channel_id=1, source_target_pairs={{1,4},{5,8},{9,12},{2,5},{6,9},{10,13},{3,6},{7,10},{11,14},{17,20... | collective-permute-start | bytes 12680 | tf_op jit(solution)/shard_map/ppermute | solution.py:21
  17.6 1.9 %collective-permute-start.6 = (bf16[2,8,2,128]{3,1,2,0:T(8,128)(2,1)S(1)}, bf16[2,8,2,128]{3,1,2,0:T(8,128)(2,1)S(1)}, u32[]{:S(2)}, u32[]{:S(2)}) collective-permute-start(bf16[2,8,2,128]{3,1,2,0:T(8,128)(2,1)S(1)} %get-tuple-element.8), channel_id=1, source_target_pairs={{1,0},{5,4},{9,8},{13,12},{2,1},{6,5},{10,9},{14,13},{3,2},{7,6},{... | collective-permute-start | bytes 24584 | tf_op jit(solution)/shard_map/ppermute | solution.py:21
  19.5 1.9 %collective-permute-start.3 = (bf16[2,8,16,66]{3,1,2,0:T(8,128)(2,1)S(1)}, bf16[2,8,16,66]{3,1,2,0:T(8,128)(2,1)S(1)}, u32[]{:S(2)}, u32[]{:S(2)}) collective-permute-start(bf16[2,8,16,66]{3,1,2,0:T(8,128)(2,1)S(1)} %slice.35), channel_id=1, source_target_pairs={{0,4},{4,8},{8,12},{1,5},{5,9},{9,13},{2,6},{6,10},{10,14},{3,7},{... | collective-permute-start | bytes 101384 | tf_op jit(solution)/shard_map/ppermute | solution.py:21
  21.5 0.9 %copy.12.q_ref = f32[288,256]{1,0:T(8,128)} copy(f32[288,256]{0,1:T(8,128)S(1)} %broadcast_bitcast_fusion) | data formatting | bytes 589824 | tf_op jit(solution)/shard_map/tile | solution.py:221
  22.4 0.7 %copy.13.agg_ref = f32[27,256]{1,0:T(8,128)} copy(f32[27,256]{0,1:T(8,128)S(1)} %broadcast_bitcast_fusion.1) | data formatting | bytes 55296 | tf_op jit(solution)/shard_map/tile | solution.py:223
  23.1 0.1 reshape.22
  23.1 0.1 copy.11
  23.2 0.7 %tile.35.bias_ref = f32[4,256]{1,0:T(4,128)} reshape(f32[4,32,8]{2,1,0:T(8,128)S(1)} %tile.34) | data formatting | bytes 8192 | tf_op jit(solution)/shard_map/tile | solution.py:222
  24.0 2.0 %collective-permute-done.3 = bf16[2,8,16,66]{3,1,2,0:T(8,128)(2,1)S(1)} collective-permute-done((bf16[2,8,16,66]{3,1,2,0:T(8,128)(2,1)S(1)}, bf16[2,8,16,66]{3,1,2,0:T(8,128)(2,1)S(1)}, u32[]{:S(2)}, u32[]{:S(2)}) %collective-permute-start.3) | collective-permute-done | bytes 33824 | tf_op jit(solution)/shard_map/ppermute | solution.py:21
  25.9 0.1 maximum_bitcast_fusion
  26.1 0.1 copy.9
  26.2 0.8 %pad_convert_fusion.pt_ref = f32[2,224,256]{2,1,0:T(8,128)} fusion(bf16[2,196,160]{2,1,0:T(8,128)(2,1)S(1)} %copy.9), kind=kLoop, calls=%fused_computation | loop fusion | flops 114688 | bytes 584192 | tf_op jit(solution)/shard_map/jit(_pad)/pad | solution.py:216
  27.0 13.1 %shard_map.46 = f32[16,128]{1,0:T(8,128)} custom-call(f32[2,224,256]{2,1,0:T(8,128)} %pad_convert_fusion.pt_ref, f32[288,256]{1,0:T(8,128)} %copy.12.q_ref, f32[4,256]{1,0:T(4,128)} %tile.35.bias_ref, f32[27,256]{1,0:T(8,128)} %copy.13.agg_ref), custom_call_target="tpu_custom_call" | custom-call | tf_op jit(solution)/shard_map/pallas_call | solution.py:224
  (18 shorter events, 0.1 us)
Async XLA Ops:
  0.0 21.5 %copy-start = (f32[8,27]{1,0:T(8,128)S(1)}, f32[8,27]{1,0:T(8,128)}, u32[]{:S(2)}) copy-start(f32[8,27]{1,0:T(8,128)} %param.7) | copy-start | bytes 2596
  1.0 22.9 %collective-permute-start = (bf16[2,8,2,66]{3,1,2,0:T(8,128)(2,1)S(1)}, bf16[2,8,2,66]{3,1,2,0:T(8,128)(2,1)S(1)}, u32[]{:S(2)}, u32[]{:S(2)}) collective-permute-start(bf16[2,8,2,66]{3,1,2,0:T(8,128)(2,1)S(1)} %get-tuple-element.5), channel_id=1, source_target_pairs={{0,5},{4,9},{8,13},{1,6},{5,10},{9,14},{2,7},{6,11},{10,15},{16,21... | collective-permute-start | bytes 12680 | tf_op jit(solution)/shard_map/ppermute | solution.py:21
  4.0 20.0 %collective-permute-start.1 = (bf16[2,8,2,128]{3,1,2,0:T(8,128)(2,1)S(1)}, bf16[2,8,2,128]{3,1,2,0:T(8,128)(2,1)S(1)}, u32[]{:S(2)}, u32[]{:S(2)}) collective-permute-start(bf16[2,8,2,128]{3,1,2,0:T(8,128)(2,1)S(1)} %get-tuple-element.7), channel_id=1, source_target_pairs={{0,1},{4,5},{8,9},{12,13},{1,2},{5,6},{9,10},{13,14},{2,3},{6,7},{... | collective-permute-start | bytes 24584 | tf_op jit(solution)/shard_map/ppermute | solution.py:21
  5.9 7.4 %copy-start.1 = (bf16[32,72]{1,0:T(8,128)(2,1)S(1)}, bf16[32,72]{1,0:T(8,128)(2,1)}, u32[]{:S(2)}) copy-start(bf16[32,72]{1,0:T(8,128)(2,1)} %param.5) | copy-start | bytes 13828
  5.9 7.9 %collective-permute-start.2 = (bf16[2,8,2,2]{3,1,2,0:T(8,128)(2,1)S(1)}, bf16[2,8,2,2]{3,1,2,0:T(8,128)(2,1)S(1)}, u32[]{:S(2)}, u32[]{:S(2)}) collective-permute-start(bf16[2,8,2,2]{3,1,2,0:T(8,128)(2,1)S(1)} %get-tuple-element.9), channel_id=1, source_target_pairs={{4,1},{8,5},{12,9},{5,2},{9,6},{13,10},{6,3},{10,7},{14,11},{20,17... | collective-permute-start | bytes 392 | tf_op jit(solution)/shard_map/ppermute | solution.py:21
  7.9 9.7 %collective-permute-start.7 = (bf16[2,8,2,2]{3,1,2,0:T(8,128)(2,1)S(1)}, bf16[2,8,2,2]{3,1,2,0:T(8,128)(2,1)S(1)}, u32[]{:S(2)}, u32[]{:S(2)}) collective-permute-start(bf16[2,8,2,2]{3,1,2,0:T(8,128)(2,1)S(1)} %get-tuple-element.10), channel_id=1, source_target_pairs={{5,0},{9,4},{13,8},{6,1},{10,5},{14,9},{7,2},{11,6},{15,10},{21,16... | collective-permute-start | bytes 392 | tf_op jit(solution)/shard_map/ppermute | solution.py:21
  11.4 8.1 %collective-permute-start.4 = (bf16[2,8,16,2]{3,1,2,0:T(8,128)(2,1)S(1)}, bf16[2,8,16,2]{3,1,2,0:T(8,128)(2,1)S(1)}, u32[]{:S(2)}, u32[]{:S(2)}) collective-permute-start(bf16[2,8,16,2]{3,1,2,0:T(8,128)(2,1)S(1)} %bitcast.16), channel_id=1, source_target_pairs={{4,0},{8,4},{12,8},{5,1},{9,5},{13,9},{6,2},{10,6},{14,10},{7,3},{... | collective-permute-start | bytes 3080 | tf_op jit(solution)/shard_map/ppermute | solution.py:21
  13.8 10.1 %collective-permute-start.5 = (bf16[2,8,2,66]{3,1,2,0:T(8,128)(2,1)S(1)}, bf16[2,8,2,66]{3,1,2,0:T(8,128)(2,1)S(1)}, u32[]{:S(2)}, u32[]{:S(2)}) collective-permute-start(bf16[2,8,2,66]{3,1,2,0:T(8,128)(2,1)S(1)} %get-tuple-element.6), channel_id=1, source_target_pairs={{1,4},{5,8},{9,12},{2,5},{6,9},{10,13},{3,6},{7,10},{11,14},{17,20... | collective-permute-start | bytes 12680 | tf_op jit(solution)/shard_map/ppermute | solution.py:21
  17.6 6.3 %collective-permute-start.6 = (bf16[2,8,2,128]{3,1,2,0:T(8,128)(2,1)S(1)}, bf16[2,8,2,128]{3,1,2,0:T(8,128)(2,1)S(1)}, u32[]{:S(2)}, u32[]{:S(2)}) collective-permute-start(bf16[2,8,2,128]{3,1,2,0:T(8,128)(2,1)S(1)} %get-tuple-element.8), channel_id=1, source_target_pairs={{1,0},{5,4},{9,8},{13,12},{2,1},{6,5},{10,9},{14,13},{3,2},{7,6},{... | collective-permute-start | bytes 24584 | tf_op jit(solution)/shard_map/ppermute | solution.py:21
  19.5 6.4 %collective-permute-start.3 = (bf16[2,8,16,66]{3,1,2,0:T(8,128)(2,1)S(1)}, bf16[2,8,16,66]{3,1,2,0:T(8,128)(2,1)S(1)}, u32[]{:S(2)}, u32[]{:S(2)}) collective-permute-start(bf16[2,8,16,66]{3,1,2,0:T(8,128)(2,1)S(1)} %slice.35), channel_id=1, source_target_pairs={{0,4},{4,8},{8,12},{1,5},{5,9},{9,13},{2,6},{6,10},{10,14},{3,7},{... | collective-permute-start | bytes 101384 | tf_op jit(solution)/shard_map/ppermute | solution.py:21
  22.4 0.7 %copy-start.2 = (f32[32]{0:T(128)S(1)}, f32[32]{0:T(128)}, u32[]{:S(2)}) copy-start(f32[32]{0:T(128)} %param.6) | copy-start | bytes 388

commit v2 on v1

--- a/solution.py
+++ b/solution.py
@@ -11,37 +11,110 @@
 BAND = 4
 
 
-def shifted(shard, axes, sizes, steps):
-    pairs = []
-    for r in range(sizes[1]):
-        for c in range(sizes[0]):
-            to_r, to_c = r - steps[0], c - steps[1]
-            if 0 <= to_r < sizes[1] and 0 <= to_c < sizes[0]:
-                pairs.append((c * sizes[1] + r, to_c * sizes[1] + to_r))
-    return lax.ppermute(shard, axes, pairs)
-
-
-def body(shape, pt_ref, q_ref, bias_ref, agg_ref, out_ref, wc, amat, lf, rf, cost, acc, score):
+MESH = pl.DeviceIdType.MESH
+STEPS = ((0, 1), (0, -1), (1, 0), (-1, 0), (1, 1), (1, -1), (-1, 1), (-1, -1))
+
+
+def body(
+    shape, tr_ref, edge_ref, weight_ref, bias_in, agg_in, out_ref,
+    pt, wc, amat, lf, rf, cost, acc, score, near0, near1, far, lines, send_sem, recv_sem,
+):
     rows, cols, groups, per, cin = shape
     lanes = wc.shape[2] // per
     lead = D + 8
     span = rf.shape[1]
     tiles = lanes // 128
-    total_rows = rows * lax.axis_size("row")
-    total_cols = cols * lax.axis_size("col")
-    top = lax.axis_index("row") * rows - 1
-    left = lax.axis_index("col") * cols
+    rows_axis, cols_axis = lax.axis_size("row"), lax.axis_size("col")
+    my_row, my_col = lax.axis_index("row"), lax.axis_index("col")
+    total_rows = rows * rows_axis
+    total_cols = cols * cols_axis
+    top = my_row * rows - 1
+    left = my_col * cols
+    reach = near1.shape[0]
+
+    def exists(step):
+        r, c = my_row + step[0], my_col + step[1]
+        return (r >= 0) & (r < rows_axis) & (c >= 0) & (c < cols_axis)
+
+    def device(step):
+        return {"row": my_row + step[0], "col": my_col + step[1]}
+
+    barrier = pltpu.get_barrier_semaphore()
+    for step in STEPS:
+
+        @pl.when(exists(step))
+        def _(step=step):
+            pl.semaphore_signal(barrier, inc=1, device_id=device(step), device_id_type=MESH)
+
+    tall = 1 + (my_row > 0).astype(jnp.int32) + (my_row < rows_axis - 1).astype(jnp.int32)
+    wide = 1 + (my_col > 0).astype(jnp.int32) + (my_col < cols_axis - 1).astype(jnp.int32)
+    pl.semaphore_wait(barrier, tall * wide - 1)
+
+    plan = [
+        ((0, 1), tr_ref.at[1, pl.ds(cols - reach, reach), :], near1),
+        ((0, 1), tr_ref.at[0, pl.ds(cols - 16, 16), :], near0),
+        ((0, -1), tr_ref.at[:, pl.ds(0, 16), :], far),
+    ]
+    for r in (1, -1):
+        side = 0 if r == 1 else 1
+        for c in (0, 1, -1):
+            plan.append(((r, c), edge_ref.at[1 - side], lines.at[side, 1 - c]))
+    copies = []
+    for k, (step, source, target) in enumerate(plan):
+        copy = pltpu.make_async_remote_copy(
+            src_ref=source,
+            dst_ref=target,
+            send_sem=send_sem.at[k],
+            recv_sem=recv_sem.at[k],
+            device_id=device(step),
+            device_id_type=MESH,
+        )
+        copies.append((step, copy))
+
+        @pl.when(exists(step))
+        def _(copy=copy):
+            copy.start()
+
+        @pl.when(jnp.logical_not(exists((-step[0], -step[1]))))
+        def _(target=target):
+            target[...] = jnp.zeros(target.shape, target.dtype)
+
+    spread_at = lax.broadcasted_iota(jnp.int32, (groups * per, lanes), 1) % groups * per
+    spread_from = lax.broadcasted_iota(jnp.int32, (groups * per, lanes), 0)
+    tn = (((0,), (0,)), ((), ()))
+    weight = weight_ref[...].astype(jnp.float32)
+    q, bias = [], []
+    for ch in range(per):
+        spread = (spread_from == spread_at + ch).astype(jnp.float32)
+        q.append(
+            lax.dot_general(weight, spread, tn, preferred_element_type=jnp.float32)
+        )
+        bias.append(
+            jnp.dot(
+                bias_in[...], spread,
+                precision=lax.Precision.HIGHEST, preferred_element_type=jnp.float32,
+            )
+        )
+    one = (
+        lax.broadcasted_iota(jnp.int32, (groups, lanes), 0)
+        == lax.broadcasted_iota(jnp.int32, (groups, lanes), 1) % groups
+    ).astype(jnp.float32)
+    agg = lax.dot_general(
+        agg_in[...], one, tn,
+        precision=lax.Precision.HIGHEST, preferred_element_type=jnp.float32,
+    )
 
     lane_row = lax.broadcasted_iota(jnp.int32, (cin, lanes), 1) // groups
+    order = list(range(2, rows + 2)) + [0, 1, rows + 2, rows + 3]
     for step_x in range(3):
         for ch in range(per):
             taps = []
             for step_y in range(3):
-                base = ((step_y * 3 + step_x) * per + ch) * cin
-                taps.append(q_ref[base : base + cin, :])
+                base = (step_y * 3 + step_x) * cin
+                taps.append(q[ch][base : base + cin, :])
             for pair in range((rows + 4) // 2):
                 halves = []
-                for line in (2 * pair, 2 * pair + 1):
+                for line in order[2 * pair : 2 * pair + 2]:
                     value = jnp.zeros((cin, lanes), jnp.float32)
                     for step_y in range(3):
                         value = jnp.where(lane_row == line - step_y, taps[step_y], value)
@@ -62,23 +135,54 @@
             value = jnp.zeros((rows, lanes), jnp.float32)
             for step_y in range(3):
                 k = 9 * step_d + 3 * step_y + step_x
-                value = jnp.where(off == step_y, agg_ref[k : k + 1, :], value)
+                value = jnp.where(off == step_y, agg[k : k + 1, :], value)
             high = value.astype(jnp.bfloat16)
             low = (value - high.astype(jnp.float32)).astype(jnp.bfloat16)
             at = (step_d * 3 + step_x) * 2 * rows
             amat[at : at + rows, :] = high
             amat[at + rows : at + 2 * rows, :] = low
 
+    for step, copy in copies:
+
+        @pl.when(exists((-step[0], -step[1])))
+        def _(copy=copy):
+            copy.wait_recv()
+
+    base = 16 + D
+    main = rows * cin
+    pt[1, base - reach : base, 0:main] = near1[...].astype(jnp.float32)
+    pt[0, base - 16 : base, 0:main] = near0[...].astype(jnp.float32)
+    pt[:, base : base + cols, 0:main] = tr_ref[...].astype(jnp.float32)
+    pt[:, base + cols : base + cols + 16, 0:main] = far[...].astype(jnp.float32)
+    half = 2 * cin
+    for image in range(2):
+        for place in range(3):
+            block = jnp.concatenate(
+                [
+                    lines[side, place, image * half : (image + 1) * half, :].astype(jnp.float32)
+                    for side in range(2)
+                ]
+                + [jnp.zeros((lanes - main - 2 * half, cols), jnp.float32)],
+                axis=0,
+            )
+            block = block.T
+            if place == 0:
+                pt[image, base - reach : base, main:] = block[cols - reach :, :]
+            elif place == 1:
+                pt[image, base : base + cols, main:] = block
+            else:
+                pt[image, base + cols : base + cols + 16, main:] = block[:16, :]
+
     def features(image, first, count, store, scale):
         row_ids = left + first - lead + lax.broadcasted_iota(jnp.int32, (count, lanes), 0)
         line = top + lax.broadcasted_iota(jnp.int32, (count, lanes), 1) // groups
         keep = (row_ids >= 0) & (row_ids < total_cols) & (line >= 0) & (line < total_rows)
         parts = [
-            pt_ref[image, 7 + step_x + first : 7 + step_x + first + count, :].astype(jnp.bfloat16)
+            pt[image, 7 + step_x + first : 7 + step_x + first + count, :].astype(jnp.bfloat16)
             for step_x in range(3)
         ]
         for ch in range(per):
-            summed = jnp.broadcast_to(bias_ref[ch : ch + 1, :], (count, lanes))
+            summed = jnp.broadcast_to(bias[ch], (count, lanes))
             total = None
             for step_x in range(3):
                 term = jnp.dot(
@@ -192,41 +296,31 @@
     total, moment = lax.fori_loop(0, D, weigh, (zero, zero), unroll=4)
     out_ref[...] = moment / total / D
 
+    for step, copy in copies:
+
+        @pl.when(exists(step))
+        def _(copy=copy):
+            copy.wait_send()
+
 
 def on_device(images, conv_weight, conv_bias, agg_weight):
     cin, rows, cols = images.shape[1:]
     groups = agg_weight.shape[0]
     per = conv_weight.shape[0] // groups
-    lanes = -(-max((rows + 2) * groups, (rows + 4) * cin) // 128) * 128
+    main = rows * cin
+    lanes = main + 128
     span = cols + D + 16
-    sizes = (lax.axis_size("col"), lax.axis_size("row"))
-    pictures = images.astype(jnp.bfloat16)
-    move = functools.partial(shifted, axes=("col", "row"), sizes=sizes)
-    wide = D + 2
-    grid = []
-    for r, lines in ((-1, slice(rows - 2, rows)), (0, slice(0, rows)), (1, slice(0, 2))):
-        line = []
-        for c, columns in ((-1, slice(cols - wide, cols)), (0, slice(0, cols)), (1, slice(0, 2))):
-            piece = pictures[:, :, lines, columns]
-            line.append(piece if r == 0 and c == 0 else move(piece, steps=(r, c)))
-        grid.append(jnp.concatenate(line, axis=3))
-    ext = jnp.concatenate(grid, axis=2)
-    pt = ext.transpose(0, 3, 2, 1).reshape(2, ext.shape[3], (rows + 4) * cin).astype(jnp.float32)
-    ahead = 16 + D - wide
-    pt = jnp.pad(
-        pt, ((0, 0), (ahead, span + 16 - ahead - pt.shape[1]), (0, lanes - pt.shape[2]))
-    )
-    repeat = lanes // groups
-    q = conv_weight.reshape(groups, per, 9, cin).transpose(2, 1, 3, 0).astype(jnp.float32)
-    q = jnp.tile(q.reshape(9 * per * cin, groups), (1, repeat))
-    bias = jnp.tile(conv_bias.reshape(groups, per).T, (1, repeat))
-    agg = jnp.tile(agg_weight.T, (1, repeat))
+    reach = -(-(D + 2) // 16) * 16
+    pictures = images.astype(jnp.bfloat16).transpose(0, 2, 1, 3)
+    tr = pictures.reshape(2, main, cols).transpose(0, 2, 1)
+    edges = jnp.stack([pictures[:, :2], pictures[:, rows - 2 :]]).reshape(2, 4 * cin, cols)
     return pl.pallas_call(
         functools.partial(body, (rows, cols, groups, per, cin)),
         out_shape=jax.ShapeDtypeStruct((rows, cols), jnp.float32),
-        in_specs=[pl.BlockSpec(memory_space=pltpu.VMEM)] * 4,
+        in_specs=[pl.BlockSpec(memory_space=pltpu.VMEM)] * 5,
         out_specs=pl.BlockSpec(memory_space=pltpu.VMEM),
         scratch_shapes=[
+            pltpu.VMEM((2, span + 16, lanes), jnp.float32),
             pltpu.VMEM((3, lanes, per * lanes), jnp.bfloat16),
             pltpu.VMEM((18 * rows, lanes), jnp.bfloat16),
             pltpu.VMEM((per * (lanes // 128), cols + 16, 128), jnp.float32),
@@ -234,8 +328,15 @@
             pltpu.VMEM((D, cols, lanes), jnp.bfloat16),
             pltpu.VMEM((3, D + 2, rows, cols), jnp.float32),
             pltpu.VMEM((D, rows, cols), jnp.float32),
+            pltpu.VMEM((16, main), jnp.bfloat16),
+            pltpu.VMEM((reach, main), jnp.bfloat16),
+            pltpu.VMEM((2, 16, main), jnp.bfloat16),
+            pltpu.VMEM((2, 3, 4 * cin, cols), jnp.bfloat16),
+            pltpu.SemaphoreType.DMA((9,)),
+            pltpu.SemaphoreType.DMA((9,)),
         ],
-    )(pt, q, bias, agg)
+        compiler_params=pltpu.CompilerParams(collective_id=0, has_side_effects=True),
+    )(tr, edges, conv_weight, conv_bias[None], agg_weight)
 
 
 def solution(mesh):

time: 40.5 us -> 23.7 us (0.59)
  the two profiles are of different devices: /device:TPU:18 before, /device:TPU:0 now
where the time goes in v2:
time: 23.7 us; the launch traced here: 23.5 us
  Pallas kernels  19.9 us (84%)
  local copies, waits for them, and re-layouts  2.98 us (13%)
  other arithmetic  0.6 us (3%)
    pallas_call x1, Pallas kernels, on_device(): pl.pallas_call(functools.partial(body, (rows, cols, groups, per, cin)), o...  19.9 us
    unnamed x2, local copies, waits for them, and re-layouts  2.25 us
    reshape x1, local copies, waits for them, and re-layouts, on_device(): tr = pictures.reshape(2, main, cols).transpose(0, 2, 1)  0.73 us
    another operation x1, other arithmetic, on_device(): jnp.stack([pictures[:, :2], pictures[:, rows - 2:]])  0.6 us

profile of v2, /device:TPU:0, one launch (start us, length us, event | category | flops | bytes accessed | tf_op | source)
XLA Modules:
  0.0 23.5 jit_solution(7888719298688499525)
XLA Ops:
  0.0 0.9 %copy.15 = bf16[2,8,16,128]{3,1,2,0:T(8,128)(2,1)S(1)} copy(f32[2,8,16,128]{3,2,1,0:T(8,128)} %param.4) | data formatting | bytes 196608 | tf_op args[0]
  1.0 0.6 %pad_maximum_fusion.edge_ref = bf16[2,32,128]{2,1,0:T(8,128)(2,1)} fusion(bf16[1,32,128]{2,1,0:T(8,128)(2,1)S(1)} %bitcast.14, bf16[1,32,128]{2,1,0:T(8,128)(2,1)S(1)} %bitcast.13), kind=kLoop, calls=%fused_computation.3 | loop fusion | flops 8192 | bytes 32768 | tf_op jit(solution)/shard_map/stack | solution.py:316
  1.6 0.7 %copy.9 = bf16[2,128,128]{1,2,0:T(8,128)(2,1)} copy(bf16[2,128,128]{2,1,0:T(8,128)(2,1)S(1)} %bitcast.11) | data formatting | bytes 131072 | tf_op jit(solution)/shard_map/reshape | solution.py:315
  2.3 19.9 %shard_map.46 = f32[16,128]{1,0:T(8,128)} custom-call(bf16[2,128,128]{2,1,0:T(8,128)(2,1)} %bitcast.12, bf16[2,32,128]{2,1,0:T(8,128)(2,1)} %pad_maximum_fusion.edge_ref, bf16[32,72]{1,0:T(8,128)(2,1)} %weight_ref.1, f32[1,32]{1,0:T(1,128)} %bitcast.15, f32[8,27]{1,0:T(8,128)} %agg_in.1), custom_call_target="tpu_custom_call" | custom-call | tf_op jit(solution)/shard_map/pallas_call | solution.py:317
  22.2 1.3 %copy.17 = f32[16,128]{1,0:T(8,128)} copy(f32[16,128]{1,0:T(8,128)} %shard_map.46) | data formatting | bytes 16384
  (1 shorter events, 0.0 us)

commit v3 on v2

--- a/solution.py
+++ b/solution.py
@@ -8,7 +8,6 @@
 from jax.sharding import PartitionSpec as P
 
 D = 64
-BAND = 4
 
 
 MESH = pl.DeviceIdType.MESH
@@ -17,7 +16,7 @@
 
 def body(
     shape, tr_ref, edge_ref, weight_ref, bias_in, agg_in, out_ref,
-    pt, wc, amat, lf, rf, cost, acc, score, near0, near1, far, lines, send_sem, recv_sem,
+    pt, wc, amat, lf, rf, raw, cost, acc, score, near0, near1, far, lines, send_sem, recv_sem,
 ):
     rows, cols, groups, per, cin = shape
     lanes = wc.shape[2] // per
@@ -31,6 +30,15 @@
     top = my_row * rows - 1
     left = my_col * cols
     reach = near1.shape[0]
+    skew = 128 // (2 * groups)
+
+    def row_of(lane):
+        beside = jnp.where((lane // groups) % 2 == 0, 0, rows + 1)
+        return jnp.where(lane < rows * groups, lane // groups + 1, beside)
+
+    def skew_of(lane):
+        return (lane - rows * groups) // (2 * groups)
+
 
     def exists(step):
         r, c = my_row + step[0], my_col + step[1]
@@ -104,7 +112,7 @@
         precision=lax.Precision.HIGHEST, preferred_element_type=jnp.float32,
     )
 
-    lane_row = lax.broadcasted_iota(jnp.int32, (cin, lanes), 1) // groups
+    lane_row = row_of(lax.broadcasted_iota(jnp.int32, (cin, lanes), 1))
     order = list(range(2, rows + 2)) + [0, 1, rows + 2, rows + 3]
     for step_x in range(3):
         for ch in range(per):
@@ -126,10 +134,10 @@
     if used < lanes:
         wc[:, used:, :] = jnp.zeros((3, lanes - used, per * lanes), jnp.bfloat16)
 
-    off = (
-        lax.broadcasted_iota(jnp.int32, (rows, lanes), 1) // groups
-        - lax.broadcasted_iota(jnp.int32, (rows, lanes), 0)
-    )
+    lane = lax.broadcasted_iota(jnp.int32, (rows, lanes), 1)
+    off = row_of(lane) - lax.broadcasted_iota(jnp.int32, (rows, lanes), 0)
+    group_main = rows * groups
+    part_of = skew_of(lane)
     for step_d in range(3):
         for step_x in range(3):
             value = jnp.zeros((rows, lanes), jnp.float32)
@@ -139,8 +147,12 @@
             high = value.astype(jnp.bfloat16)
             low = (value - high.astype(jnp.float32)).astype(jnp.bfloat16)
             at = (step_d * 3 + step_x) * 2 * rows
-            amat[at : at + rows, :] = high
-            amat[at + rows : at + 2 * rows, :] = low
+            for v, value in enumerate((high, low)):
+                begin = at + v * rows
+                amat[0, begin : begin + rows, :] = value[:, :group_main]
+                for ds in range(skew):
+                    own = jnp.where(part_of == ds, value.astype(jnp.float32), 0.0)
+                    amat[1 + ds, begin : begin + rows, :] = own[:, group_main:].astype(jnp.bfloat16)
 
     for step, copy in copies:
 
@@ -175,7 +187,7 @@
 
     def features(image, first, count, store, scale):
         row_ids = left + first - lead + lax.broadcasted_iota(jnp.int32, (count, lanes), 0)
-        line = top + lax.broadcasted_iota(jnp.int32, (count, lanes), 1) // groups
+        line = top + row_of(lax.broadcasted_iota(jnp.int32, (count, lanes), 1))
         keep = (row_ids >= 0) & (row_ids < total_cols) & (line >= 0) & (line < total_rows)
         parts = [
             pt[image, 7 + step_x + first : 7 + step_x + first + count, :].astype(jnp.bfloat16)
@@ -201,25 +213,14 @@
     features(0, lead - 8, cols + 16, lf, 1.0 / per)
     features(1, 0, span, rf, 1.0)
 
-    for tile in range(tiles):
-        for chunk in range(cols // 16):
-            lefts = [
-                lf[ch * tiles + tile, 8 + chunk * 16 : 24 + chunk * 16, :] for ch in range(per)
-            ]
-
-            def layer(d, carry):
-                total = None
-                for ch in range(per):
-                    term = (
-                        lefts[ch] * rf[ch * tiles + tile, pl.ds(lead + chunk * 16 - d, 16), :]
-                    )
-                    total = term if total is None else total + term
-                cost[d, chunk * 16 : (chunk + 1) * 16, tile * 128 : (tile + 1) * 128] = (
-                    total.astype(jnp.bfloat16)
-                )
-                return carry
-
-            lax.fori_loop(0, D, layer, 0, unroll=4)
+    apart = skew_of(lax.broadcasted_iota(jnp.int32, (span, 128), 1) + group_main)
+    for ch in range(per):
+        raw[ch, 0:8, :] = jnp.zeros((8, 128), jnp.float32)
+        value = rf[ch * tiles + 1, :, :]
+        raw[ch, 8 : 8 + span, :] = value
+        for ds in range(1, skew):
+            value = jnp.where(apart == ds, raw[ch, 8 - ds : 8 - ds + span, :], value)
+        rf[ch * tiles + 1, :, :] = value
 
     edges = []
     for at, begin in ((7, lead - D), (8 + cols, lead + cols - D + 1)):
@@ -234,7 +235,10 @@
         edges.append(jnp.concatenate(parts, axis=1))
     edge = jnp.concatenate(edges, axis=0)
     nt = (((1,), (1,)), ((), ()))
-    side = lax.dot_general(amat[...], edge, nt, preferred_element_type=jnp.float32)
+    main_a = amat[0]
+    side = lax.dot_general(
+        jnp.concatenate([main_a, amat[1]], axis=1), edge, nt, preferred_element_type=jnp.float32
+    )
     place = lax.broadcasted_iota(jnp.int32, (rows, 2 * D), 1)
     within = jnp.where(place >= D, place - D, place)
     border = None
@@ -252,23 +256,47 @@
 
     acc[...] = jnp.zeros_like(acc)
 
+    def product(tile, chunk, d):
+        total = None
+        for ch in range(per):
+            k = ch * tiles + tile
+            term = (
+                lf[k, 8 + chunk * 16 : 24 + chunk * 16, :]
+                * rf[k, pl.ds(lead + chunk * 16 - d, 16), :]
+            )
+            total = term if total is None else total + term
+        return total.astype(jnp.bfloat16)
+
     def band(block, carry):
-        d0 = block * BAND
-        stack = cost[pl.ds(d0, BAND), :, :].reshape(BAND * cols, lanes)
-        got = lax.dot_general(amat[...], stack, nt, preferred_element_type=jnp.float32)
-        for step_x in range(3):
-            for o in range(BAND + 2):
-                value = acc[step_x, d0 + o, :, :]
-                for step_d in range(3):
-                    j = o + step_d - 2
-                    if 0 <= j < BAND:
+        d0 = block * 2 * skew
+        beside = []
+        for p in range(2):
+            for chunk in range(cols // 16):
+                beside.append(product(1, chunk, d0 + p * skew))
+        cost[0, :, group_main:] = jnp.concatenate(beside, axis=0)
+        held = {}
+        for ds in range(skew):
+            for p in range(2):
+                for chunk in range(cols // 16):
+                    at = p * cols + chunk * 16
+                    cost[ds, at : at + 16, :group_main] = product(0, chunk, d0 + p * skew + ds)
+            stack = jnp.concatenate([cost[ds, :, :group_main], cost[0, :, group_main:]], axis=1)
+            weights = jnp.concatenate([amat[0], amat[1 + ds]], axis=1)
+            got = lax.dot_general(weights, stack, nt, preferred_element_type=jnp.float32)
+            for step_x in range(3):
+                for p in range(2):
+                    for step_d in range(3):
                         at = (step_d * 3 + step_x) * 2 * rows
-                        value += got[at : at + rows, j * cols : (j + 1) * cols]
-                        value += got[at + rows : at + 2 * rows, j * cols : (j + 1) * cols]
-                acc[step_x, d0 + o, :, :] = value
+                        columns = slice(p * cols, (p + 1) * cols)
+                        value = got[at : at + rows, columns] + got[at + rows : at + 2 * rows, columns]
+                        key = (step_x, p, ds + 2 - step_d)
+                        held[key] = held[key] + value if key in held else value
+                    done = [ds] if ds < skew - 1 else [ds, ds + 1, ds + 2]
+                    for o in done:
+                        acc[step_x, d0 + p * skew + o, :, :] += held.pop((step_x, p, o))
         return carry
 
-    lax.fori_loop(0, D // BAND, band, 0)
+    lax.fori_loop(0, D // (2 * skew), band, 0)
 
     lane = lax.broadcasted_iota(jnp.int32, (rows, cols), 1)
 
@@ -322,10 +350,11 @@
         scratch_shapes=[
             pltpu.VMEM((2, span + 16, lanes), jnp.float32),
             pltpu.VMEM((3, lanes, per * lanes), jnp.bfloat16),
-            pltpu.VMEM((18 * rows, lanes), jnp.bfloat16),
+            pltpu.VMEM((1 + 64 // groups, 18 * rows, 128), jnp.bfloat16),
             pltpu.VMEM((per * (lanes // 128), cols + 16, 128), jnp.float32),
             pltpu.VMEM((per * (lanes // 128), span, 128), jnp.float32),
-            pltpu.VMEM((D, cols, lanes), jnp.bfloat16),
+            pltpu.VMEM((per, span + 8, 128), jnp.float32),
+            pltpu.VMEM((64 // groups, 2 * cols, lanes), jnp.bfloat16),
             pltpu.VMEM((3, D + 2, rows, cols), jnp.float32),
             pltpu.VMEM((D, rows, cols), jnp.float32),
             pltpu.VMEM((16, main), jnp.bfloat16),

time: 23.7 us -> 19.5 us (0.82)
  Pallas kernels: 19.9 us -> 15.7 us
    pallas_call x1, Pallas kernels: 19.9 us -> 15.7 us  [on_device(): pl.pallas_call(functools.partial(body, (rows, cols, groups, per, cin)), o...]
where the time goes in v3:
time: 19.5 us; the launch traced here: 19.3 us
  Pallas kernels  15.7 us (81%)
  local copies, waits for them, and re-layouts  2.98 us (15%)
  other arithmetic  0.6 us (3%)
    pallas_call x1, Pallas kernels, on_device(): pl.pallas_call(functools.partial(body, (rows, cols, groups, per, cin)), o...  15.7 us
    unnamed x2, local copies, waits for them, and re-layouts  2.25 us
    reshape x1, local copies, waits for them, and re-layouts, on_device(): tr = pictures.reshape(2, main, cols).transpose(0, 2, 1)  0.73 us
    another operation x1, other arithmetic, on_device(): jnp.stack([pictures[:, :2], pictures[:, rows - 2:]])  0.6 us

profile of v3, /device:TPU:0, one launch (start us, length us, event | category | flops | bytes accessed | tf_op | source)
XLA Modules:
  0.0 19.3 jit_solution(14622806249663178195)
XLA Ops:
  0.0 0.9 %copy.15 = bf16[2,8,16,128]{3,1,2,0:T(8,128)(2,1)S(1)} copy(f32[2,8,16,128]{3,2,1,0:T(8,128)} %param.4) | data formatting | bytes 196608 | tf_op args[0]
  1.0 0.6 %pad_maximum_fusion.edge_ref = bf16[2,32,128]{2,1,0:T(8,128)(2,1)} fusion(bf16[1,32,128]{2,1,0:T(8,128)(2,1)S(1)} %bitcast.14, bf16[1,32,128]{2,1,0:T(8,128)(2,1)S(1)} %bitcast.13), kind=kLoop, calls=%fused_computation.3 | loop fusion | flops 8192 | bytes 32768 | tf_op jit(solution)/shard_map/stack | solution.py:344
  1.6 0.7 %copy.9 = bf16[2,128,128]{1,2,0:T(8,128)(2,1)} copy(bf16[2,128,128]{2,1,0:T(8,128)(2,1)S(1)} %bitcast.11) | data formatting | bytes 131072 | tf_op jit(solution)/shard_map/reshape | solution.py:343
  2.3 15.7 %shard_map.46 = f32[16,128]{1,0:T(8,128)} custom-call(bf16[2,128,128]{2,1,0:T(8,128)(2,1)} %bitcast.12, bf16[2,32,128]{2,1,0:T(8,128)(2,1)} %pad_maximum_fusion.edge_ref, bf16[32,72]{1,0:T(8,128)(2,1)} %weight_ref.1, f32[1,32]{1,0:T(1,128)} %bitcast.15, f32[8,27]{1,0:T(8,128)} %agg_in.1), custom_call_target="tpu_custom_call" | custom-call | tf_op jit(solution)/shard_map/pallas_call | solution.py:345
  18.0 1.3 %copy.17 = f32[16,128]{1,0:T(8,128)} copy(f32[16,128]{1,0:T(8,128)} %shard_map.46) | data formatting | bytes 16384
  (1 shorter events, 0.0 us)

commit v4 on v3

--- a/solution.py
+++ b/solution.py
@@ -15,8 +15,8 @@
 
 
 def body(
-    shape, tr_ref, edge_ref, weight_ref, bias_in, agg_in, out_ref,
-    pt, wc, amat, lf, rf, raw, cost, acc, score, near0, near1, far, lines, send_sem, recv_sem,
+    shape, images_ref, weight_ref, bias_in, agg_in, out_ref,
+    pt, wc, amat, lf, rf, raw, cost, acc, score, tr_ref, edge_ref, near0, near1, far, lines, send_sem, recv_sem,
 ):
     rows, cols, groups, per, cin = shape
     lanes = wc.shape[2] // per
@@ -46,6 +46,16 @@
 
     def device(step):
         return {"row": my_row + step[0], "col": my_col + step[1]}
+
+    main = rows * cin
+    for image in range(2):
+        flat = images_ref[image].reshape(main, cols)
+        tr_ref[image] = flat.T.astype(jnp.bfloat16)
+        for side, first in ((0, 0), (1, rows - 2)):
+            pair = [images_ref[image, :, first + y, :] for y in range(2)]
+            edge_ref[side, image * 2 * cin : (image + 1) * 2 * cin, :] = jnp.concatenate(
+                pair, axis=0
+            ).astype(jnp.bfloat16)
 
     barrier = pltpu.get_barrier_semaphore()
     for step in STEPS:
@@ -112,22 +122,30 @@
         precision=lax.Precision.HIGHEST, preferred_element_type=jnp.float32,
     )
 
-    lane_row = row_of(lax.broadcasted_iota(jnp.int32, (cin, lanes), 1))
-    order = list(range(2, rows + 2)) + [0, 1, rows + 2, rows + 3]
+    lane_row = row_of(lax.broadcasted_iota(jnp.int32, (rows, lanes), 1))
+    line_off = lane_row - lax.broadcasted_iota(jnp.int32, (rows, lanes), 0)
+    near_row = lane_row[:cin]
     for step_x in range(3):
         for ch in range(per):
+            columns = slice(ch * lanes, (ch + 1) * lanes)
             taps = []
             for step_y in range(3):
                 base = (step_y * 3 + step_x) * cin
                 taps.append(q[ch][base : base + cin, :])
-            for pair in range((rows + 4) // 2):
+            for c in range(cin):
+                value = jnp.zeros((rows, lanes), jnp.float32)
+                for step_y in range(3):
+                    value = jnp.where(line_off == 2 - step_y, taps[step_y][c : c + 1, :], value)
+                wc[step_x, c * rows : (c + 1) * rows, columns] = value.astype(jnp.bfloat16)
+            for pair in range(2):
                 halves = []
-                for line in order[2 * pair : 2 * pair + 2]:
+                for line in ((0, 1), (rows + 2, rows + 3))[pair]:
                     value = jnp.zeros((cin, lanes), jnp.float32)
                     for step_y in range(3):
-                        value = jnp.where(lane_row == line - step_y, taps[step_y], value)
+                        value = jnp.where(near_row == line - step_y, taps[step_y], value)
                     halves.append(value)
-                wc[step_x, pair * 2 * cin : (pair + 1) * 2 * cin, ch * lanes : (ch + 1) * lanes] = (
+                begin = main + pair * 2 * cin
+                wc[step_x, begin : begin + 2 * cin, columns] = (
                     jnp.concatenate(halves, axis=0).astype(jnp.bfloat16)
                 )
     used = (rows + 4) * cin
@@ -161,7 +179,6 @@
             copy.wait_recv()
 
     base = 16 + D
-    main = rows * cin
     pt[1, base - reach : base, 0:main] = near1[...].astype(jnp.float32)
     pt[0, base - 16 : base, 0:main] = near0[...].astype(jnp.float32)
     pt[:, base : base + cols, 0:main] = tr_ref[...].astype(jnp.float32)
@@ -313,7 +330,7 @@
         score[d, :, :] = value
         return jnp.maximum(best, value)
 
-    best = lax.fori_loop(0, D, finish, jnp.full((rows, cols), -jnp.inf, jnp.float32), unroll=4)
+    best = lax.fori_loop(0, D, finish, jnp.full((rows, cols), -jnp.inf, jnp.float32), unroll=16)
 
     def weigh(d, carry):
         total, moment = carry
@@ -321,7 +338,7 @@
         return total + weight, moment + weight * d.astype(jnp.float32)
 
     zero = jnp.zeros((rows, cols), jnp.float32)
-    total, moment = lax.fori_loop(0, D, weigh, (zero, zero), unroll=4)
+    total, moment = lax.fori_loop(0, D, weigh, (zero, zero), unroll=16)
     out_ref[...] = moment / total / D
 
     for step, copy in copies:
@@ -339,13 +356,10 @@
     lanes = main + 128
     span = cols + D + 16
     reach = -(-(D + 2) // 16) * 16
-    pictures = images.astype(jnp.bfloat16).transpose(0, 2, 1, 3)
-    tr = pictures.reshape(2, main, cols).transpose(0, 2, 1)
-    edges = jnp.stack([pictures[:, :2], pictures[:, rows - 2 :]]).reshape(2, 4 * cin, cols)
     return pl.pallas_call(
         functools.partial(body, (rows, cols, groups, per, cin)),
         out_shape=jax.ShapeDtypeStruct((rows, cols), jnp.float32),
-        in_specs=[pl.BlockSpec(memory_space=pltpu.VMEM)] * 5,
+        in_specs=[pl.BlockSpec(memory_space=pltpu.VMEM)] * 4,
         out_specs=pl.BlockSpec(memory_space=pltpu.VMEM),
         scratch_shapes=[
             pltpu.VMEM((2, span + 16, lanes), jnp.float32),
@@ -357,6 +371,8 @@
             pltpu.VMEM((64 // groups, 2 * cols, lanes), jnp.bfloat16),
             pltpu.VMEM((3, D + 2, rows, cols), jnp.float32),
             pltpu.VMEM((D, rows, cols), jnp.float32),
+            pltpu.VMEM((2, cols, main), jnp.bfloat16),
+            pltpu.VMEM((2, 4 * cin, cols), jnp.bfloat16),
             pltpu.VMEM((16, main), jnp.bfloat16),
             pltpu.VMEM((reach, main), jnp.bfloat16),
             pltpu.VMEM((2, 16, main), jnp.bfloat16),
@@ -365,7 +381,7 @@
             pltpu.SemaphoreType.DMA((9,)),
         ],
         compiler_params=pltpu.CompilerParams(collective_id=0, has_side_effects=True),
-    )(tr, edges, conv_weight, conv_bias[None], agg_weight)
+    )(images, conv_weight, conv_bias[None], agg_weight)
 
 
 def solution(mesh):

time: 19.5 us -> 16.5 us (0.85)
  local copies, waits for them, and re-layouts: 2.98 us -> 1.3 us
  Pallas kernels: 15.7 us -> 15 us
  other arithmetic: 0.6 us -> 0 us
    unnamed x2 -> x1, local copies, waits for them, and re-layouts: 2.25 us -> 1.3 us
    reshape x1 -> x0, local copies, waits for them, and re-layouts: 0.73 us -> none  [on_device(): tr = pictures.reshape(2, main, cols).transpose(0, 2, 1)]
    pallas_call x1, Pallas kernels: 15.7 us -> 15 us  [on_device(): pl.pallas_call(functools.partial(body, (rows, cols, groups, per, cin)), o...]
    another operation x1 -> x0, other arithmetic: 0.6 us -> none  [on_device(): jnp.stack([pictures[:, :2], pictures[:, rows - 2:]])]
where the time goes in v4:
time: 16.5 us; the launch traced here: 16.3 us
  Pallas kernels  15 us (91%)
  local copies, waits for them, and re-layouts  1.3 us (8%)
    pallas_call x1, Pallas kernels, on_device(): pl.pallas_call(functools.partial(body, (rows, cols, groups, per, cin)), o...  15 us
    unnamed x1, local copies, waits for them, and re-layouts  1.3 us

profile of v4, /device:TPU:0, one launch (start us, length us, event | category | flops | bytes accessed | tf_op | source)
XLA Modules:
  0.0 16.3 jit_solution(16419296657173848872)
XLA Ops:
  0.0 15.0 %shard_map.46 = f32[16,128]{1,0:T(8,128)} custom-call(f32[2,8,16,128]{3,2,1,0:T(8,128)} %images_ref.1, bf16[32,72]{1,0:T(8,128)(2,1)} %weight_ref.1, f32[1,32]{1,0:T(1,128)} %bitcast.1, f32[8,27]{1,0:T(8,128)} %agg_in.1), custom_call_target="tpu_custom_call" | custom-call | tf_op jit(solution)/shard_map/pallas_call | solution.py:359
  15.0 1.3 %copy.6 = f32[16,128]{1,0:T(8,128)} copy(f32[16,128]{1,0:T(8,128)} %shard_map.46) | data formatting | bytes 16384

commit v5 on v4

--- a/solution.py
+++ b/solution.py
@@ -47,6 +47,13 @@
     def device(step):
         return {"row": my_row + step[0], "col": my_col + step[1]}
 
+    barrier = pltpu.get_barrier_semaphore()
+    for step in STEPS:
+
+        @pl.when(exists(step))
+        def _(step=step):
+            pl.semaphore_signal(barrier, inc=1, device_id=device(step), device_id_type=MESH)
+
     main = rows * cin
     for image in range(2):
         flat = images_ref[image].reshape(main, cols)
@@ -57,12 +64,50 @@
                 pair, axis=0
             ).astype(jnp.bfloat16)
 
-    barrier = pltpu.get_barrier_semaphore()
-    for step in STEPS:
-
-        @pl.when(exists(step))
-        def _(step=step):
-            pl.semaphore_signal(barrier, inc=1, device_id=device(step), device_id_type=MESH)
+    spread_at = lax.broadcasted_iota(jnp.int32, (groups * per, lanes), 1) % groups * per
+    spread_from = lax.broadcasted_iota(jnp.int32, (groups * per, lanes), 0)
+    tn = (((0,), (0,)), ((), ()))
+    weight = weight_ref[...].astype(jnp.float32)
+    q, bias = [], []
+    for ch in range(per):
+        spread = (spread_from == spread_at + ch).astype(jnp.float32)
+        q.append(
+            lax.dot_general(weight, spread, tn, preferred_element_type=jnp.float32)
+        )
+        bias.append(
+            jnp.dot(
+                bias_in[...], spread,
+                precision=lax.Precision.HIGHEST, preferred_element_type=jnp.float32,
+            )
+        )
+    one = (
+        lax.broadcasted_iota(jnp.int32, (groups, lanes), 0)
+        == lax.broadcasted_iota(jnp.int32, (groups, lanes), 1) % groups
+    ).astype(jnp.float32)
+    agg = lax.dot_general(
+        agg_in[...], one, tn,
+        precision=lax.Precision.HIGHEST, preferred_element_type=jnp.float32,
+    )
+
+    lane = lax.broadcasted_iota(jnp.int32, (rows, lanes), 1)
+    off = row_of(lane) - lax.broadcasted_iota(jnp.int32, (rows, lanes), 0)
+    group_main = rows * groups
+    part_of = skew_of(lane)
+    for step_d in range(3):
+        for step_x in range(3):
+            value = jnp.zeros((rows, lanes), jnp.float32)
+            for step_y in range(3):
+                k = 9 * step_d + 3 * step_y + step_x
+                value = jnp.where(off == step_y, agg[k : k + 1, :], value)
+            high = value.astype(jnp.bfloat16)
+            low = (value - high.astype(jnp.float32)).astype(jnp.bfloat16)
+            at = (step_d * 3 + step_x) * 2 * rows
+            for v, value in enumerate((high, low)):
+                begin = at + v * rows
+                amat[0, begin : begin + rows, :] = value[:, :group_main]
+                for ds in range(skew):
+                    own = jnp.where(part_of == ds, value.astype(jnp.float32), 0.0)
+                    amat[1 + ds, begin : begin + rows, :] = own[:, group_main:].astype(jnp.bfloat16)
 
     tall = 1 + (my_row > 0).astype(jnp.int32) + (my_row < rows_axis - 1).astype(jnp.int32)
     wide = 1 + (my_col > 0).astype(jnp.int32) + (my_col < cols_axis - 1).astype(jnp.int32)
@@ -96,31 +141,6 @@
         @pl.when(jnp.logical_not(exists((-step[0], -step[1]))))
         def _(target=target):
             target[...] = jnp.zeros(target.shape, target.dtype)
-
-    spread_at = lax.broadcasted_iota(jnp.int32, (groups * per, lanes), 1) % groups * per
-    spread_from = lax.broadcasted_iota(jnp.int32, (groups * per, lanes), 0)
-    tn = (((0,), (0,)), ((), ()))
-    weight = weight_ref[...].astype(jnp.float32)
-    q, bias = [], []
-    for ch in range(per):
-        spread = (spread_from == spread_at + ch).astype(jnp.float32)
-        q.append(
-            lax.dot_general(weight, spread, tn, preferred_element_type=jnp.float32)
-        )
-        bias.append(
-            jnp.dot(
-                bias_in[...], spread,
-                precision=lax.Precision.HIGHEST, preferred_element_type=jnp.float32,
-            )
-        )
-    one = (
-        lax.broadcasted_iota(jnp.int32, (groups, lanes), 0)
-        == lax.broadcasted_iota(jnp.int32, (groups, lanes), 1) % groups
-    ).astype(jnp.float32)
-    agg = lax.dot_general(
-        agg_in[...], one, tn,
-        precision=lax.Precision.HIGHEST, preferred_element_type=jnp.float32,
-    )
 
     lane_row = row_of(lax.broadcasted_iota(jnp.int32, (rows, lanes), 1))
     line_off = lane_row - lax.broadcasted_iota(jnp.int32, (rows, lanes), 0)
@@ -152,25 +172,9 @@
     if used < lanes:
         wc[:, used:, :] = jnp.zeros((3, lanes - used, per * lanes), jnp.bfloat16)
 
-    lane = lax.broadcasted_iota(jnp.int32, (rows, lanes), 1)
-    off = row_of(lane) - lax.broadcasted_iota(jnp.int32, (rows, lanes), 0)
-    group_main = rows * groups
-    part_of = skew_of(lane)
-    for step_d in range(3):
-        for step_x in range(3):
-            value = jnp.zeros((rows, lanes), jnp.float32)
-            for step_y in range(3):
-                k = 9 * step_d + 3 * step_y + step_x
-                value = jnp.where(off == step_y, agg[k : k + 1, :], value)
-            high = value.astype(jnp.bfloat16)
-            low = (value - high.astype(jnp.float32)).astype(jnp.bfloat16)
-            at = (step_d * 3 + step_x) * 2 * rows
-            for v, value in enumerate((high, low)):
-                begin = at + v * rows
-                amat[0, begin : begin + rows, :] = value[:, :group_main]
-                for ds in range(skew):
-                    own = jnp.where(part_of == ds, value.astype(jnp.float32), 0.0)
-                    amat[1 + ds, begin : begin + rows, :] = own[:, group_main:].astype(jnp.bfloat16)
+    acc[...] = jnp.zeros_like(acc)
+    base = 16 + D
+    pt[:, base : base + cols, 0:main] = tr_ref[...].astype(jnp.float32)
 
     for step, copy in copies:
 
@@ -181,7 +185,6 @@
     base = 16 + D
     pt[1, base - reach : base, 0:main] = near1[...].astype(jnp.float32)
     pt[0, base - 16 : base, 0:main] = near0[...].astype(jnp.float32)
-    pt[:, base : base + cols, 0:main] = tr_ref[...].astype(jnp.float32)
     pt[:, base + cols : base + cols + 16, 0:main] = far[...].astype(jnp.float32)
     half = 2 * cin
     for image in range(2):
@@ -270,8 +273,6 @@
         elif step_d == 2:
             value = jnp.where(within == 0, 0.0, pltpu.roll(value, 1, 1))
         border = value if border is None else border + value
-
-    acc[...] = jnp.zeros_like(acc)
 
     def product(tile, chunk, d):
         total = None

time: 16.5 us -> 16.2 us (0.982)
  Pallas kernels: 15 us -> 14.7 us
    pallas_call x1, Pallas kernels: 15 us -> 14.7 us  [on_device(): pl.pallas_call(functools.partial(body, (rows, cols, groups, per, cin)), o...]
where the time goes in v5:
time: 16.2 us; the launch traced here: 16 us
  Pallas kernels  14.7 us (91%)
  local copies, waits for them, and re-layouts  1.3 us (8%)
    pallas_call x1, Pallas kernels, on_device(): pl.pallas_call(functools.partial(body, (rows, cols, groups, per, cin)), o...  14.7 us
    unnamed x1, local copies, waits for them, and re-layouts  1.3 us

profile of v5, /device:TPU:0, one launch (start us, length us, event | category | flops | bytes accessed | tf_op | source)
XLA Modules:
  0.0 16.0 jit_solution(16028092692727779737)
XLA Ops:
  0.0 14.7 %shard_map.46 = f32[16,128]{1,0:T(8,128)} custom-call(f32[2,8,16,128]{3,2,1,0:T(8,128)} %images_ref.1, bf16[32,72]{1,0:T(8,128)(2,1)} %weight_ref.1, f32[1,32]{1,0:T(1,128)} %bitcast.1, f32[8,27]{1,0:T(8,128)} %agg_in.1), custom_call_target="tpu_custom_call" | custom-call | tf_op jit(solution)/shard_map/pallas_call | solution.py:360
  14.7 1.3 %copy.6 = f32[16,128]{1,0:T(8,128)} copy(f32[16,128]{1,0:T(8,128)} %shard_map.46) | data formatting | bytes 16384

commit v6 on v5

--- a/solution.py
+++ b/solution.py
@@ -314,7 +314,7 @@
                         acc[step_x, d0 + p * skew + o, :, :] += held.pop((step_x, p, o))
         return carry
 
-    lax.fori_loop(0, D // (2 * skew), band, 0)
+    lax.fori_loop(0, D // (2 * skew), band, 0, unroll=2)
 
     lane = lax.broadcasted_iota(jnp.int32, (rows, cols), 1)
 

time: 16.2 us -> 15.8 us (0.975)
  Pallas kernels: 14.7 us -> 14.3 us
    pallas_call x1, Pallas kernels: 14.7 us -> 14.3 us  [on_device(): pl.pallas_call(functools.partial(body, (rows, cols, groups, per, cin)), o...]
where the time goes in v6:
time: 15.8 us; the launch traced here: 15.6 us
  Pallas kernels  14.3 us (91%)
  local copies, waits for them, and re-layouts  1.3 us (8%)
    pallas_call x1, Pallas kernels, on_device(): pl.pallas_call(functools.partial(body, (rows, cols, groups, per, cin)), o...  14.3 us
    unnamed x1, local copies, waits for them, and re-layouts  1.3 us

profile of v6, /device:TPU:0, one launch (start us, length us, event | category | flops | bytes accessed | tf_op | source)
XLA Modules:
  0.0 15.6 jit_solution(12312569958420926759)
XLA Ops:
  0.0 14.3 %shard_map.46 = f32[16,128]{1,0:T(8,128)} custom-call(f32[2,8,16,128]{3,2,1,0:T(8,128)} %images_ref.1, bf16[32,72]{1,0:T(8,128)(2,1)} %weight_ref.1, f32[1,32]{1,0:T(1,128)} %bitcast.1, f32[8,27]{1,0:T(8,128)} %agg_in.1), custom_call_target="tpu_custom_call" | custom-call | tf_op jit(solution)/shard_map/pallas_call | solution.py:360
  14.3 1.3 %copy.6 = f32[16,128]{1,0:T(8,128)} copy(f32[16,128]{1,0:T(8,128)} %shard_map.46) | data formatting | bytes 16384
